TPU v7x, 32 devices: a whole 2x2x4 slice. The times are simulated.
32 devices in a mesh: rep: 4 (over z), dp: 8 (over y, x, core).
Axes of the slice: x: 2, y: 2, z: 4, core: 2. Of those that a mesh axis runs over, the one named last changes fastest.
Arguments:
- history: bfloat16 [8, 8192, 2048], P(None, ('rep', 'dp')), may hold values from -6 to 6
- stream_mix: float32 [8192, 32], P(('rep', 'dp')), may hold values from -3 to 3
- lengths: int32 [32], P(('rep', 'dp')), may hold values from 1 to 256, 5120 in all
- w_query: bfloat16 [2048, 2048], P('dp'), may hold values from -0.1875 to 0.1875
- w_key: bfloat16 [2048, 2048], P('dp'), may hold values from -0.1875 to 0.1875
- w_value: bfloat16 [2048, 2048], P('dp'), may hold values from -0.125 to 0.125
- w_output: bfloat16 [2048, 2048], P('dp'), may hold values from -0.5 to 0.5
- gain_query: bfloat16 [2048], P('dp'), may hold values from 0.25 to 1.75
- gain_key: bfloat16 [2048], P('dp'), may hold values from 0.25 to 1.75
- gain_value: bfloat16 [2048], P('dp'), may hold values from 0.25 to 1.75
- w_up: bfloat16 [2048, 8192], P('dp'), may hold values from -0.125 to 0.125
- w_down: bfloat16 [8192, 2048], P('dp'), may hold values from -0.0625 to 0.0625
- gain_mlp: bfloat16 [2048], P('dp'), may hold values from 0.25 to 1.75
- w_mix_in: bfloat16 [2048, 32], P('dp'), may hold values from -0.125 to 0.125
- w_mix_out: bfloat16 [32, 36], P('dp'), may hold values from -1 to 1
- gain_mix: bfloat16 [2048], P('dp'), may hold values from 0.25 to 1.75
- grad_block: bfloat16 [8192, 2048], P(('rep', 'dp')), may hold values from -6 to 6
- grad_next: float32 [8192, 36], P(('rep', 'dp')), may hold values from -6 to 6
Outputs:
- block_output: bfloat16 [8192, 2048], P(('rep', 'dp'))
- next_mix: float32 [8192, 36], P(('rep', 'dp'))
- grad_history: bfloat16 [8, 8192, 2048], P(None, ('rep', 'dp'))
- grad_stream_mix: float32 [8192, 32], P(('rep', 'dp'))
- grad_w_query: float32 [2048, 2048], P('dp')
- grad_w_key: float32 [2048, 2048], P('dp')
- grad_w_value: float32 [2048, 2048], P('dp')
- grad_w_output: float32 [2048, 2048], P('dp')
- grad_gain_query: float32 [2048], P('dp')
- grad_gain_key: float32 [2048], P('dp')
- grad_gain_value: float32 [2048], P('dp')
- grad_w_up: float32 [2048, 8192], P('dp')
- grad_w_down: float32 [8192, 2048], P('dp')
- grad_gain_mlp: float32 [2048], P('dp')
- grad_w_mix_in: float32 [2048, 32], P('dp')
- grad_w_mix_out: float32 [32, 36], P('dp')
- grad_gain_mix: float32 [2048], P('dp')
Inputs may be any that keep to these rules, and one draw needn't show every extreme that they name: `lengths`: each slot's sequence fills it from its start; in every draw some slot holds exactly 256 valid tokens.
All inputs are finite; a program needn't handle non-finite values. No bound on the sum of `lengths` on one device may be relied on, other than what follows from the above.
Results may differ from a plain program's by a relative error of at most 0.02.
Values may be sent and summed in bfloat16 or wider, within the bound.
No kernel may reach another device: no remote copies, remote signals or barrier semaphores. Data moves between devices by JAX's collectives and lax.ppermute only.
A program may use at most 448 MiB of HBM per device.

v0:
```python
import jax
import jax.numpy as jnp
from jax import lax
from jax.sharding import PartitionSpec as P

HEADS = 16
HD = 128
HIST = 8
STREAMS = 4


def rms_scale(value, gain):
    return value * lax.rsqrt(jnp.mean(value * value, axis=-1, keepdims=True) + 1e-06) * gain


def rotary(heads_value):
    row_count = heads_value.shape[0]
    half_size = heads_value.shape[-1] // 2
    freqs = 10000.0 ** (-jnp.arange(half_size, dtype=jnp.float32) / half_size)
    angles = jnp.arange(row_count, dtype=jnp.float32)[:, None] * freqs[None, :]
    cos_part = jnp.cos(angles)[:, None, :]
    sin_part = jnp.sin(angles)[:, None, :]
    first_half = heads_value[..., :half_size]
    second_half = heads_value[..., half_size:]
    return jnp.concatenate(
        [
            first_half * cos_part - second_half * sin_part,
            second_half * cos_part + first_half * sin_part,
        ],
        axis=-1,
    )


def norm_back(value, gain, grad_normed):
    unused, pullback = jax.vjp(rms_scale, value, gain)
    return pullback(grad_normed)


def gelu_back(value, grad_value):
    unused, pullback = jax.vjp(jax.nn.gelu, value)
    return pullback(grad_value)[0]


def rotary_back(value, grad_value):
    unused, pullback = jax.vjp(rotary, value)
    return pullback(grad_value)[0]


def masked_scores(query_rot, keys_rot, valid_count):
    row_count = query_rot.shape[0]
    raw_scores = jnp.einsum(
        "qhe,khe->hqk", query_rot, keys_rot, preferred_element_type=jnp.float32
    ) * HD ** (-0.5)
    position = jnp.arange(row_count, dtype=jnp.int32)
    allowed = (position[None, :] <= position[:, None]) & (position[None, :] < valid_count)
    return jnp.where(allowed[None], raw_scores, -1e30)


def body(
    history,
    stream_mix,
    lengths,
    w_query,
    w_key,
    w_value,
    w_output,
    gain_query,
    gain_key,
    gain_value,
    w_up,
    w_down,
    gain_mlp,
    w_mix_in,
    w_mix_out,
    gain_mix,
    grad_block,
    grad_next,
):
    row_count = history.shape[1]
    valid_count = lengths[0]
    position = jnp.arange(row_count, dtype=jnp.int32)
    row_keep = (position < valid_count).astype(jnp.float32)[:, None]
    score_scale = HD ** (-0.5)
    full_query, full_key, full_value, full_output, full_gain_q, full_gain_k, full_gain_v = (
        lax.all_gather(w_query, "dp", axis=0, tiled=True),
        lax.all_gather(w_key, "dp", axis=0, tiled=True),
        lax.all_gather(w_value, "dp", axis=0, tiled=True),
        lax.all_gather(w_output, "dp", axis=0, tiled=True),
        lax.all_gather(gain_query, "dp", axis=0, tiled=True),
        lax.all_gather(gain_key, "dp", axis=0, tiled=True),
        lax.all_gather(gain_value, "dp", axis=0, tiled=True),
    )
    full_gain_q = full_gain_q.astype(jnp.float32)
    full_gain_k = full_gain_k.astype(jnp.float32)
    full_gain_v = full_gain_v.astype(jnp.float32)
    weights_mix = stream_mix.reshape(row_count, STREAMS, HIST)
    streams = jnp.einsum(
        "tsj,jtd->std",
        weights_mix,
        history,
        precision=lax.Precision.HIGHEST,
        preferred_element_type=jnp.float32,
    )
    normed_q = rms_scale(streams[0], full_gain_q).astype(jnp.bfloat16)
    normed_k = rms_scale(streams[1], full_gain_k).astype(jnp.bfloat16)
    normed_v = rms_scale(streams[2], full_gain_v).astype(jnp.bfloat16)
    query = jnp.dot(normed_q, full_query, preferred_element_type=jnp.float32).reshape(
        row_count, HEADS, HD
    )
    keys = jnp.dot(normed_k, full_key, preferred_element_type=jnp.float32).reshape(
        row_count, HEADS, HD
    )
    value_heads = (
        jnp.dot(normed_v, full_value, preferred_element_type=jnp.float32)
        .astype(jnp.bfloat16)
        .reshape(row_count, HEADS, HD)
    )
    query_rot = rotary(query).astype(jnp.bfloat16)
    keys_rot = rotary(keys).astype(jnp.bfloat16)
    scores = masked_scores(query_rot, keys_rot, valid_count)
    row_max = jnp.max(scores, axis=-1, keepdims=True)
    log_total = row_max + jnp.log(jnp.sum(jnp.exp(scores - row_max), axis=-1, keepdims=True))
    probs_low = jnp.exp(scores - log_total).astype(jnp.bfloat16)
    mixed = (
        jnp.einsum("hqk,khe->qhe", probs_low, value_heads, preferred_element_type=jnp.float32)
        .astype(jnp.bfloat16)
        .reshape(row_count, HEADS * HD)
    )
    hidden = streams[3] + jnp.dot(mixed, full_output, preferred_element_type=jnp.float32)
    full_up, full_down, full_gain_m = (
        lax.all_gather(w_up, "dp", axis=0, tiled=True),
        lax.all_gather(w_down, "dp", axis=0, tiled=True),
        lax.all_gather(gain_mlp, "dp", axis=0, tiled=True),
    )
    full_gain_m = full_gain_m.astype(jnp.float32)
    normed_m = rms_scale(hidden, full_gain_m).astype(jnp.bfloat16)
    upper = jnp.dot(normed_m, full_up, preferred_element_type=jnp.float32)
    active = jax.nn.gelu(upper).astype(jnp.bfloat16)
    block = hidden + jnp.dot(active, full_down, preferred_element_type=jnp.float32)
    full_mix_in, full_mix_out, full_gain_x = (
        lax.all_gather(w_mix_in, "dp", axis=0, tiled=True),
        lax.all_gather(w_mix_out, "dp", axis=0, tiled=True),
        lax.all_gather(gain_mix, "dp", axis=0, tiled=True),
    )
    full_gain_x = full_gain_x.astype(jnp.float32)
    normed_x = rms_scale(block, full_gain_x).astype(jnp.bfloat16)
    inner = jnp.dot(normed_x, full_mix_in, preferred_element_type=jnp.float32)
    inner_act = jax.nn.gelu(inner).astype(jnp.bfloat16)
    logits = jnp.dot(inner_act, full_mix_out, preferred_element_type=jnp.float32)
    block_output = (block * row_keep).astype(jnp.bfloat16)
    next_mix = logits * row_keep
    d_logits = (grad_next * row_keep).astype(jnp.bfloat16)
    grad_mix_out = jnp.einsum("tk,to->ko", inner_act, d_logits, preferred_element_type=jnp.float32)
    d_inner_act = jnp.einsum(
        "to,ko->tk", d_logits, full_mix_out, preferred_element_type=jnp.float32
    )
    d_inner = gelu_back(inner, d_inner_act).astype(jnp.bfloat16)
    grad_mix_in = jnp.einsum("td,tk->dk", normed_x, d_inner, preferred_element_type=jnp.float32)
    d_normed_x = jnp.einsum("tk,dk->td", d_inner, full_mix_in, preferred_element_type=jnp.float32)
    d_block_norm, grad_gain_x = norm_back(block, full_gain_x, d_normed_x)
    owned_mix_in, owned_mix_out, owned_gain_x = (
        lax.psum_scatter(
            grad_mix_in.astype(jnp.bfloat16), "dp", scatter_dimension=0, tiled=True
        ).astype(jnp.float32),
        lax.psum_scatter(
            grad_mix_out.astype(jnp.bfloat16), "dp", scatter_dimension=0, tiled=True
        ).astype(jnp.float32),
        lax.psum_scatter(
            grad_gain_x.astype(jnp.bfloat16), "dp", scatter_dimension=0, tiled=True
        ).astype(jnp.float32),
    )
    d_block = grad_block.astype(jnp.float32) * row_keep + d_block_norm
    back_up, back_down = (
        lax.all_gather(w_up, "dp", axis=0, tiled=True),
        lax.all_gather(w_down, "dp", axis=0, tiled=True),
    )
    d_block_low = d_block.astype(jnp.bfloat16)
    grad_down = jnp.einsum("tf,td->fd", active, d_block_low, preferred_element_type=jnp.float32)
    d_active = jnp.einsum("td,fd->tf", d_block_low, back_down, preferred_element_type=jnp.float32)
    owned_down = lax.psum_scatter(
        grad_down.astype(jnp.bfloat16), "dp", scatter_dimension=0, tiled=True
    )
    d_upper = gelu_back(upper, d_active).astype(jnp.bfloat16)
    grad_up = jnp.einsum("td,tf->df", normed_m, d_upper, preferred_element_type=jnp.float32)
    d_normed_m = jnp.einsum("tf,df->td", d_upper, back_up, preferred_element_type=jnp.float32)
    d_hidden_norm, grad_gain_m = norm_back(hidden, full_gain_m, d_normed_m)
    owned_up, owned_gain_m = (
        lax.psum_scatter(
            grad_up.astype(jnp.bfloat16), "dp", scatter_dimension=0, tiled=True
        ).astype(jnp.float32),
        lax.psum_scatter(
            grad_gain_m.astype(jnp.bfloat16), "dp", scatter_dimension=0, tiled=True
        ).astype(jnp.float32),
    )
    d_hidden = d_block + d_hidden_norm
    back_query, back_key, back_value, back_output = (
        lax.all_gather(w_query, "dp", axis=0, tiled=True),
        lax.all_gather(w_key, "dp", axis=0, tiled=True),
        lax.all_gather(w_value, "dp", axis=0, tiled=True),
        lax.all_gather(w_output, "dp", axis=0, tiled=True),
    )
    d_hidden_low = d_hidden.astype(jnp.bfloat16)
    grad_output = jnp.einsum("td,te->de", mixed, d_hidden_low, preferred_element_type=jnp.float32)
    d_mixed = (
        jnp.einsum("te,de->td", d_hidden_low, back_output, preferred_element_type=jnp.float32)
        .astype(jnp.bfloat16)
        .reshape(row_count, HEADS, HD)
    )
    probs_again = jnp.exp(masked_scores(query_rot, keys_rot, valid_count) - log_total)
    d_probs = jnp.einsum("qhe,khe->hqk", d_mixed, value_heads, preferred_element_type=jnp.float32)
    d_values = jnp.einsum(
        "hqk,qhe->khe",
        probs_again.astype(jnp.bfloat16),
        d_mixed,
        preferred_element_type=jnp.float32,
    )
    row_delta = jnp.sum(probs_again * d_probs, axis=-1, keepdims=True)
    d_scores = (probs_again * (d_probs - row_delta)).astype(jnp.bfloat16)
    d_query_rot = (
        jnp.einsum("hqk,khe->qhe", d_scores, keys_rot, preferred_element_type=jnp.float32)
        * score_scale
    )
    d_keys_rot = (
        jnp.einsum("hqk,qhe->khe", d_scores, query_rot, preferred_element_type=jnp.float32)
        * score_scale
    )
    d_query = rotary_back(query, d_query_rot).astype(jnp.bfloat16).reshape(row_count, HEADS * HD)
    d_keys = rotary_back(keys, d_keys_rot).astype(jnp.bfloat16).reshape(row_count, HEADS * HD)
    d_values = d_values.astype(jnp.bfloat16).reshape(row_count, HEADS * HD)
    grad_query = jnp.einsum("td,te->de", normed_q, d_query, preferred_element_type=jnp.float32)
    grad_key = jnp.einsum("td,te->de", normed_k, d_keys, preferred_element_type=jnp.float32)
    grad_value = jnp.einsum("td,te->de", normed_v, d_values, preferred_element_type=jnp.float32)
    d_normed_q = jnp.einsum("te,de->td", d_query, back_query, preferred_element_type=jnp.float32)
    d_normed_k = jnp.einsum("te,de->td", d_keys, back_key, preferred_element_type=jnp.float32)
    d_normed_v = jnp.einsum("te,de->td", d_values, back_value, preferred_element_type=jnp.float32)
    d_stream_q, grad_gain_q = norm_back(streams[0], full_gain_q, d_normed_q)
    d_stream_k, grad_gain_k = norm_back(streams[1], full_gain_k, d_normed_k)
    d_stream_v, grad_gain_v = norm_back(streams[2], full_gain_v, d_normed_v)
    owned_query, owned_key, owned_value, owned_output, owned_gain_q, owned_gain_k, owned_gain_v = (
        lax.psum_scatter(
            grad_query.astype(jnp.bfloat16), "dp", scatter_dimension=0, tiled=True
        ).astype(jnp.float32),
        lax.psum_scatter(
            grad_key.astype(jnp.bfloat16), "dp", scatter_dimension=0, tiled=True
        ).astype(jnp.float32),
        lax.psum_scatter(
            grad_value.astype(jnp.bfloat16), "dp", scatter_dimension=0, tiled=True
        ).astype(jnp.float32),
        lax.psum_scatter(
            grad_output.astype(jnp.bfloat16), "dp", scatter_dimension=0, tiled=True
        ).astype(jnp.float32),
        lax.psum_scatter(
            grad_gain_q.astype(jnp.bfloat16), "dp", scatter_dimension=0, tiled=True
        ).astype(jnp.float32),
        lax.psum_scatter(
            grad_gain_k.astype(jnp.bfloat16), "dp", scatter_dimension=0, tiled=True
        ).astype(jnp.float32),
        lax.psum_scatter(
            grad_gain_v.astype(jnp.bfloat16), "dp", scatter_dimension=0, tiled=True
        ).astype(jnp.float32),
    )
    d_streams = jnp.stack([d_stream_q, d_stream_k, d_stream_v, d_hidden], axis=0)
    grad_stream_mix = jnp.einsum(
        "std,jtd->tsj",
        d_streams,
        history,
        precision=lax.Precision.HIGHEST,
        preferred_element_type=jnp.float32,
    ).reshape(row_count, STREAMS * HIST)
    grad_history = jnp.einsum(
        "tsj,std->jtd",
        weights_mix,
        d_streams,
        precision=lax.Precision.HIGHEST,
        preferred_element_type=jnp.float32,
    ).astype(jnp.bfloat16)
    summed = (
        lax.psum(owned_query.astype(jnp.bfloat16), "rep").astype(jnp.float32),
        lax.psum(owned_key.astype(jnp.bfloat16), "rep").astype(jnp.float32),
        lax.psum(owned_value.astype(jnp.bfloat16), "rep").astype(jnp.float32),
        lax.psum(owned_output.astype(jnp.bfloat16), "rep").astype(jnp.float32),
        lax.psum(owned_gain_q.astype(jnp.bfloat16), "rep").astype(jnp.float32),
        lax.psum(owned_gain_k.astype(jnp.bfloat16), "rep").astype(jnp.float32),
        lax.psum(owned_gain_v.astype(jnp.bfloat16), "rep").astype(jnp.float32),
        lax.psum(owned_up.astype(jnp.bfloat16), "rep").astype(jnp.float32),
        lax.psum(owned_down, "rep").astype(jnp.float32),
        lax.psum(owned_gain_m.astype(jnp.bfloat16), "rep").astype(jnp.float32),
        lax.psum(owned_mix_in.astype(jnp.bfloat16), "rep").astype(jnp.float32),
        lax.psum(owned_mix_out.astype(jnp.bfloat16), "rep").astype(jnp.float32),
        lax.psum(owned_gain_x.astype(jnp.bfloat16), "rep").astype(jnp.float32),
    )
    return (
        block_output,
        next_mix,
        grad_history,
        grad_stream_mix,
        summed[0],
        summed[1],
        summed[2],
        summed[3],
        summed[4],
        summed[5],
        summed[6],
        summed[7],
        summed[8],
        summed[9],
        summed[10],
        summed[11],
        summed[12],
    )


def solution(mesh):
    return jax.shard_map(
        body,
        mesh=mesh,
        in_specs=(
            P(None, ("rep", "dp"), None),
            P(("rep", "dp"), None),
            P(("rep", "dp")),
            P("dp", None),
            P("dp", None),
            P("dp", None),
            P("dp", None),
            P("dp"),
            P("dp"),
            P("dp"),
            P("dp", None),
            P("dp", None),
            P("dp"),
            P("dp", None),
            P("dp", None),
            P("dp"),
            P(("rep", "dp"), None),
            P(("rep", "dp"), None),
        ),
        out_specs=(
            P(("rep", "dp"), None),
            P(("rep", "dp"), None),
            P(None, ("rep", "dp"), None),
            P(("rep", "dp"), None),
            P("dp", None),
            P("dp", None),
            P("dp", None),
            P("dp", None),
            P("dp"),
            P("dp"),
            P("dp"),
            P("dp", None),
            P("dp", None),
            P("dp"),
            P("dp", None),
            P("dp", None),
            P("dp"),
        ),
        check_vma=False,
    )
```

profile of v0, /device:TPU:0, one launch (start us, length us, event | category | flops | bytes accessed | tf_op | source)
XLA Modules:
  0.0 1863.3 jit_solution(9733515569083801879)
XLA Ops:
  12.0 10.3 all-gather.4
  22.4 8.9 all-gather.3
  31.3 7.9 all-gather
  39.2 8.9 all-gather.2
  48.1 7.9 all-gather.1
  57.1 14.6 fusion.16
  71.8 2.3 slice.40
  74.1 9.5 all-gather.5
  83.6 9.2 all_gather.56
  94.0 8.4 fusion.91
  104.3 12.2 copy.87
  116.5 7.3 all-gather.15.cloned.1.call-done
  123.8 12.3 copy.86
  136.0 6.6 fusion.43
  143.1 2.8 fusion.45
  149.9 30.2 %all-gather.13.cloned.1.call-done = bf16[2048,2048]{1,0:T(8,128)(2,1)} async-done(((bf16[256,2048]{1,0:T(8,128)(2,1)}), bf16[2048,2048]{1,0:T(8,128)(2,1)}) %all-gather.13.cloned.1.call-update) | async-done | bytes 8388624 | tf_op jit(solution)/shard_map/all_gather | solution.py:87
  180.1 6.2 fusion.36
  188.5 47.8 %all-gather.19.cloned.1.call-done = bf16[2048,2048]{1,0:T(8,128)(2,1)} async-done(((bf16[256,2048]{1,0:T(8,128)(2,1)}), bf16[2048,2048]{1,0:T(8,128)(2,1)}) %all-gather.19.cloned.1.call-update) | async-done | bytes 8388624 | tf_op jit(solution)/shard_map/all_gather | solution.py:88
  236.3 16.5 multiply_reduce_fusion.7
  252.8 146.0 %all-gather.21.cloned.1.call-done = bf16[2048,8192]{1,0:T(8,128)(2,1)} async-done(((bf16[256,8192]{1,0:T(8,128)(2,1)}), bf16[2048,8192]{1,0:T(8,128)(2,1)}) %all-gather.21.cloned.1.call-update) | async-done | bytes 33554448 | tf_op jit(solution)/shard_map/all_gather | solution.py:131
  398.8 21.3 %fusion.90 = f32[256,8192]{1,0:T(8,128)} fusion(bf16[2048,8192]{1,0:T(8,128)(2,1)} %all-gather.21.cloned.1.call-done, f32[256,2048]{1,0:T(8,128)} %get-tuple-element.120, f32[2048]{0:T(1024)S(1)} %bitcast.170, f32[256]{0:T(256)S(1)} %fusion.80), kind=kOutput, calls=%fused_computation.172 | convolution fusion | flops 8591507456 | bytes 44049408 | tf_op jit(solution)/shard_map/dot_general | solution.py:137
  420.1 141.3 %all-gather.23.cloned.1.call-done = bf16[8192,2048]{1,0:T(8,128)(2,1)} async-done(((bf16[1024,2048]{1,0:T(8,128)(2,1)}), bf16[8192,2048]{1,0:T(8,128)(2,1)}) %all-gather.23.cloned.1.call-update) | async-done | bytes 33554448 | tf_op jit(solution)/shard_map/all_gather | solution.py:132
  561.4 20.1 %multiply_reduce_fusion.6 = (f32[256]{0:T(256)S(1)}, f32[256,2048]{1,0:T(8,128)}) fusion(f32[256,2048]{1,0:T(8,128)} %get-tuple-element.120, bf16[8192,2048]{1,0:T(8,128)(2,1)} %all-gather.23.cloned.1.call-done, f32[256,8192]{1,0:T(8,128)} %fusion.90), kind=kOutput, calls=%fused_computation.82 | convolution fusion | flops 8610381824 | bytes 46138368 | tf_op jit(solution)/shard_map/dot_general | solution.py:139
  581.5 2.0 multiply_convert_fusion.3
  586.0 2.4 fusion.21
  588.4 21.4 %fusion.6 = bf16[256,8192]{1,0:T(8,128)(2,1)} fusion(f32[256,8192]{1,0:T(8,128)} %fusion.90, bf16[8192,2048]{1,0:T(8,128)(2,1)} %all-gather.23.cloned.1.call-done, f32[256,2048]{1,0:T(8,128)} %get-tuple-element.109), kind=kOutput, calls=%fused_computation.10 | convolution fusion | flops 8632401920 | bytes 48234496 | tf_op jit(solution)/shard_map/td,fd->tf/dot_general | solution.py:179
  609.8 18.0 multiply_reduce_fusion.2
  627.8 3.3 fusion.22
  631.1 1.3 copy-done.12
  632.5 6.7 convolution_convert_fusion.6
  639.2 2.7 copy.116
  641.9 3.6 convolution_convert_fusion.9
  646.5 6.6 convolution_convert_fusion.3
  653.2 4.3 multiply_reduce_fusion
  660.5 2.1 multiply_add_fusion.3
  665.0 6.7 convolution_convert_fusion.5
  671.9 1.8 add_convert_fusion
  674.7 6.6 convolution_convert_fusion.4
  681.4 7.6 convolution_convert_fusion.2
  689.1 18.8 %convolution_convert_fusion = bf16[8192,2048]{1,0:T(8,128)(2,1)} fusion(f32[256,2048]{1,0:T(8,128)} %get-tuple-element.109, f32[256,8192]{1,0:T(8,128)} %fusion.90), kind=kOutput, calls=%fused_computation | convolution fusion | flops 8626110464 | bytes 44040192 | tf_op jit(solution)/shard_map/tf,td->fd/dot_general | solution.py:178
  707.9 17.2 convolution_convert_fusion.1
  726.6 73.7 %reduce-scatter.8.cloned.1.call-done = bf16[256,2048]{1,0:T(8,128)(2,1)} async-done(((bf16[2048,2048]{1,0:T(8,128)(2,1)}), bf16[256,2048]{1,0:T(8,128)(2,1)}) %reduce-scatter.8.cloned.1.call-update) | async-done | bytes 1048592 | tf_op jit(solution)/shard_map/reduce_scatter | solution.py:240
  800.3 75.3 %reduce-scatter.10.cloned.1.call-done = bf16[256,2048]{1,0:T(8,128)(2,1)} async-done(((bf16[2048,2048]{1,0:T(8,128)(2,1)}), bf16[256,2048]{1,0:T(8,128)(2,1)}) %reduce-scatter.10.cloned.1.call-update) | async-done | bytes 1048592 | tf_op jit(solution)/shard_map/reduce_scatter | solution.py:243
  875.7 75.0 %reduce-scatter.14.cloned.1.call-done = bf16[256,2048]{1,0:T(8,128)(2,1)} async-done(((bf16[2048,2048]{1,0:T(8,128)(2,1)}), bf16[256,2048]{1,0:T(8,128)(2,1)}) %reduce-scatter.14.cloned.1.call-update) | async-done | bytes 1048592 | tf_op jit(solution)/shard_map/reduce_scatter | solution.py:249
  950.7 208.8 %reduce-scatter.18.cloned.1.call-done = bf16[1024,2048]{1,0:T(8,128)(2,1)} async-done(((bf16[8192,2048]{1,0:T(8,128)(2,1)}), bf16[1024,2048]{1,0:T(8,128)(2,1)}) %reduce-scatter.18.cloned.1.call-update) | async-done | bytes 4194320 | tf_op jit(solution)/shard_map/reduce_scatter | solution.py:180
  1159.5 209.1 %reduce-scatter.16.cloned.1.call-done = bf16[256,8192]{1,0:T(8,128)(2,1)} async-done(((bf16[2048,8192]{1,0:T(8,128)(2,1)}), bf16[256,8192]{1,0:T(8,128)(2,1)}) %reduce-scatter.16.cloned.1.call-update) | async-done | bytes 4194320 | tf_op jit(solution)/shard_map/reduce_scatter | solution.py:188
  1371.4 8.0 multiply_reduce_fusion.3
  1379.4 8.1 fusion.33
  1387.6 4.5 fusion.29
  1392.1 23.5 %all-reduce.10 = (bf16[2048]{0:T(1024)(128)(2,1)S(1)}, bf16[2048]{0:T(1024)(128)(2,1)S(1)}, bf16[2048]{0:T(1024)(128)(2,1)S(1)}, bf16[2048]{0:T(1024)(128)(2,1)S...) all-reduce(bf16[2048]{0:T(1024)(128)(2,1)S(1)} %get-tuple-element.7, ...), channel_id=6, replica_groups=mesh['rep'=4,'dp'=8] {'dp'}, use_global_device_ids=true, to_apply=%region_22.23.clone | all-reduce | flops 11392 | bytes 45568
  1418.7 3.2 fusion.24
  1422.8 1.7 fusion.23
  1425.3 3.5 copy-done.8
  1428.8 26.5 %fusion.7 = f32[256,4,8]{2,1,0:T(4,128)S(1)} fusion(f32[4,256,2048]{2,1,0:T(8,128)S(1)} %pad_maximum_fusion, bf16[8,256,2048]{2,1,0:T(8,128)(2,1)S(1)} %bitcast.155), kind=kOutput, calls=%fused_computation.18 | convolution fusion | flops 201326592 | bytes 16809984 | tf_op jit(solution)/shard_map/std,jtd->tsj/dot_general | solution.py:263
  1456.1 26.0 %convert_bitcast_fusion = bf16[8,256,2048]{2,0,1:T(8,128)(2,1)} fusion(f32[256,4,8]{2,1,0:T(4,128)S(1)} %copy-done.18, f32[4,256,2048]{2,1,0:T(8,128)} %copy-done.8), kind=kOutput, calls=%fused_computation.12 | convolution fusion | flops 205520896 | bytes 16809984 | tf_op jit(solution)/shard_map/tsj,std->jtd/dot_general | solution.py:270
  1482.2 11.5 copy.103
  1495.3 25.7 %all-reduce.11 = (bf16[256]{0:T(256)(128)(2,1)S(1)}, bf16[256]{0:T(256)(128)(2,1)S(1)}, bf16[256]{0:T(256)(128)(2,1)S(1)}, bf16[256]{0:T(256)(128)(2,1)S(1)}, bf...) all-reduce(bf16[256]{0:T(256)(128)(2,1)S(1)} %copy-done.69, ...), channel_id=1, replica_groups=mesh['rep'=4,'dp'=8] {'rep'}, use_global_device_ids=true, to_apply=%region_23.24 | all-reduce | flops 9616 | bytes 38464 | tf_op jit(solution)/shard_map/psum | solution.py:282
  1525.0 314.0 %all-reduce.15.cloned.1.call-done = (bf16[256,2048]{1,0:T(8,128)(2,1)}, bf16[256,2048]{1,0:T(8,128)(2,1)}, bf16[256,2048]{1,0:T(8,128)(2,1)}, bf16[256,2048]{1,0...) async-done(((bf16[256,2048]{1,0:T(8,128)(2,1)}, bf16[256,2048]{1,0:T(8,128)(2,1)}, bf16[256,2048]{1,0:T(8,128)(2,1)}, bf16[256,2048]{1,0:T(8,128)(2,1)}, ...) | async-done | bytes 12582928 | tf_op jit(solution)/shard_map/psum | solution.py:278
  1839.0 2.9 convert_element_type.253
  1841.9 1.6 convert_element_type.255
  1843.4 1.6 convert_element_type.259
  1845.0 1.6 convert_element_type.261
  1847.5 4.4 convert_element_type.269
  1851.8 4.4 convert_element_type.271
  (263 shorter events, 39.6 us)
Async XLA Ops:
  7.2 97.1 %all-gather.17.cloned.1.call-start = ((), (), s32[]{:S(2)}) async-start(), calls=%async_computation.9 | async-start | bytes 9437184 | tf_op jit(solution)/shard_map/all_gather | solution.py:86
  7.9 115.9 %all-gather.15.cloned.1.call-start = ((), (), s32[]{:S(2)}) async-start(), calls=%async_computation.8 | async-start | bytes 9437184 | tf_op jit(solution)/shard_map/all_gather | solution.py:85
  8.7 171.4 %all-gather.13.cloned.1.call-start = ((), (), s32[]{:S(2)}) async-start(), calls=%async_computation.7 | async-start | bytes 9437184 | tf_op jit(solution)/shard_map/all_gather | solution.py:87
  9.4 226.9 %all-gather.19.cloned.1.call-start = ((), (), s32[]{:S(2)}) async-start(), calls=%async_computation.10 | async-start | bytes 9437184 | tf_op jit(solution)/shard_map/all_gather | solution.py:88
  10.0 388.8 %all-gather.21.cloned.1.call-start = ((), (), s32[]{:S(2)}) async-start(), calls=%async_computation.11 | async-start | bytes 37748736 | tf_op jit(solution)/shard_map/all_gather | solution.py:131
  10.6 45.4 %copy-start.44 = (f32[256,32]{0,1:T(8,128)S(1)}, f32[256,32]{0,1:T(8,128)}, u32[]{:S(2)}) copy-start(f32[256,32]{0,1:T(8,128)} %param.19) | copy-start | bytes 98308
  10.6 550.8 %all-gather.23.cloned.1.call-start = ((), (), s32[]{:S(2)}) async-start(), calls=%async_computation.12 | async-start | bytes 37748736 | tf_op jit(solution)/shard_map/all_gather | solution.py:132
  11.2 715.4 %reduce-scatter.12.cloned.1.call-start = ((), (), s32[]{:S(2)}) async-start(), calls=%async_computation.15 | async-start | bytes 9437184 | tf_op jit(solution)/shard_map/reduce_scatter | solution.py:246
  48.1 45.9 %copy-start.42 = (f32[8,1,256]{2,1,0:T(1,128)}, f32[8,1,256]{2,1,0:T(1,128)S(1)}, u32[]{:S(2)}) copy-start(f32[8,1,256]{2,1,0:T(1,128)S(1)} %convert_element_type.282) | copy-start | bytes 24580
  71.8 11.8 copy-start.52
  74.1 19.9 %copy-start.9 = (f32[1,256,2048]{2,0,1:T(1,128)}, f32[1,256,2048]{2,0,1:T(1,128)S(1)}, u32[]{:S(2)}) copy-start(f32[1,256,2048]{2,0,1:T(1,128)S(1)} %slice.40) | copy-start | bytes 6291460
  94.0 8.5 copy-start.55
  94.0 8.5 copy-start.53
  103.8 12.7 copy-start.57
  103.8 38.9 %copy-start.48 = (f32[256]{0:T(256)}, f32[256]{0:T(256)S(1)}, u32[]{:S(2)}) copy-start(f32[256]{0:T(256)S(1)} %fusion.78) | copy-start | bytes 3076
  136.0 6.7 copy-start.1
  136.0 7.0 copy-start.15
  180.1 7.2 copy-start.6
  188.5 64.3 %copy-start.14 = (bf16[16,128,256]{2,1,0:T(8,128)(2,1)}, bf16[16,128,256]{2,1,0:T(8,128)(2,1)S(1)}, u32[]{:S(2)}) copy-start(bf16[16,128,256]{2,1,0:T(8,128)(2,1)S(1)} %convolution_convert_fusion.10) | copy-start | bytes 3145732
  581.5 3.1 copy-start.61
  581.5 3.1 copy-start.65
  581.5 3.1 copy-start.74
  581.5 3.2 copy-start.11
  653.1 147.2 %reduce-scatter.8.cloned.1.call-start = ((), (), s32[]{:S(2)}) async-start(), calls=%async_computation.13 | async-start | bytes 9437184 | tf_op jit(solution)/shard_map/reduce_scatter | solution.py:240
  653.2 4.3 copy-start.7
  671.7 204.0 %reduce-scatter.10.cloned.1.call-start = ((), (), s32[]{:S(2)}) async-start(), calls=%async_computation.14 | async-start | bytes 9437184 | tf_op jit(solution)/shard_map/reduce_scatter | solution.py:243
  671.9 2.8 copy-start.16
  681.4 269.3 %reduce-scatter.14.cloned.1.call-start = ((), (), s32[]{:S(2)}) async-start(), calls=%async_computation.16 | async-start | bytes 9437184 | tf_op jit(solution)/shard_map/reduce_scatter | solution.py:249
  689.0 470.5 %reduce-scatter.18.cloned.1.call-start = ((), (), s32[]{:S(2)}) async-start(), calls=%async_computation.18 | async-start | bytes 37748736 | tf_op jit(solution)/shard_map/reduce_scatter | solution.py:180
  707.9 660.8 %reduce-scatter.16.cloned.1.call-start = ((), (), s32[]{:S(2)}) async-start(), calls=%async_computation.17 | async-start | bytes 37748736 | tf_op jit(solution)/shard_map/reduce_scatter | solution.py:188
  725.1 770.1 %reduce-scatter.20.cloned.1.call-start = ((), (), s32[]{:S(2)}) async-start(), calls=%async_computation.19 | async-start | bytes 147456 | tf_op jit(solution)/shard_map/reduce_scatter | solution.py:162
  726.1 1112.9 %all-reduce.15.cloned.1.call-start = ((), (), s32[]{:S(2)}) async-start(), calls=%async_computation.20 | async-start | bytes 25165824 | tf_op jit(solution)/shard_map/psum | solution.py:278
  1368.6 2.7 copy-start.36
  1371.3 8.0 copy-start.3
  1371.3 8.0 copy-start.22
  1371.3 16.2 slice-start.2
  1379.4 8.1 copy-start.10
  1379.4 8.1 slice-start.3
  1379.4 8.1 copy-start.24
  1379.4 8.1 copy-start.43
  1379.4 8.1 copy-start.54
  1387.5 4.5 copy-start.51
  1387.6 31.0 %copy-start.60 = (f32[256]{0:T(256)S(1)}, f32[256]{0:T(256)}, u32[]{:S(2)}) copy-start(f32[256]{0:T(256)} %copy-done.59) | copy-start | bytes 3076
  1387.6 31.0 %copy-start.58 = (f32[256]{0:T(256)S(1)}, f32[256]{0:T(256)}, u32[]{:S(2)}) copy-start(f32[256]{0:T(256)} %copy-done.57) | copy-start | bytes 3076
  1387.6 31.1 %copy-start.56 = (f32[256]{0:T(256)S(1)}, f32[256]{0:T(256)}, u32[]{:S(2)}) copy-start(f32[256]{0:T(256)} %copy-done.55) | copy-start | bytes 3076
  1418.7 3.2 copy-start.4
  1418.7 3.5 copy-start.33
  1418.7 4.1 copy-start.34
  1418.7 4.1 copy-start.50
  1422.8 6.0 slice-start
  1424.5 4.2 slice-start.1
  1425.3 3.5 copy-start.8
  1428.8 27.4 %copy-start.18 = (f32[256,4,8]{2,1,0:T(4,128)S(1)}, f32[256,4,8]{2,1,0:T(4,128)}, u32[]{:S(2)}) copy-start(f32[256,4,8]{2,1,0:T(4,128)} %copy-done.17) | copy-start | bytes 98308
  1482.1 12.3 copy-start.47
  1482.1 12.3 copy-start.62
  1482.1 12.3 copy-start.67
  1482.1 13.1 copy-start.69
  1482.2 13.1 copy-start.70
  1482.2 13.1 copy-start.71
  1482.2 13.1 copy-start.72
  1482.2 13.1 copy-start.73
  1839.0 2.9 copy-start.39
  1843.4 4.0 copy-start.20
  1847.5 4.4 copy-start.19
  (36 other events, 52.0 us)
Sparse Core Ops, SparseCore 0:
  9.9 57.1 all-gather.16
  69.0 54.7 all-gather.14
  125.7 54.3 all-gather.12
  181.8 54.3 all-gather.18
  238.0 160.7 all-gather.20
  400.6 160.7 all-gather.22
  653.2 71.3 reduce-scatter.11
  729.0 71.2 reduce-scatter.7
  804.4 71.2 reduce-scatter.9
  879.4 71.2 reduce-scatter.13
  954.3 205.2 reduce-scatter.17
  1163.4 205.2 reduce-scatter.15
  1371.6 33.3 reduce-scatter.19
  1408.5 430.4 all-reduce.14
where the time goes:
time: 1870 us; the launch traced here: 1860 us
  waiting for transfers between devices  1330 us (71%)
  matrix products  286 us (15%)
  blocking collectives  112 us (6%)
  local copies, waits for them, and re-layouts  62.8 us (3%)
  other arithmetic  52.1 us (3%)
    psum x1, waiting for transfers between devices, body(): lax.psum(owned_query.astype(jnp.bfloat16), 'rep').astype(jnp.float32)  314 us
    reduce_scatter x1, waiting for transfers between devices, body(): lax.psum_scatter(grad_up.astype(jnp.bfloat16), 'dp', scatter_dimension=0,...  209 us
    reduce_scatter x1, waiting for transfers between devices, body(): lax.psum_scatter(grad_down.astype(jnp.bfloat16), 'dp', scatter_dimension=...  209 us
    all_gather x1, waiting for transfers between devices, body(): lax.all_gather(w_up, 'dp', axis=0, tiled=True)  146 us
    all_gather x1, waiting for transfers between devices, body(): lax.all_gather(w_down, 'dp', axis=0, tiled=True)  141 us
    reduce_scatter x1, waiting for transfers between devices, body(): lax.psum_scatter(grad_key.astype(jnp.bfloat16), 'dp', scatter_dimension=0...  75.3 us
    reduce_scatter x1, waiting for transfers between devices, body(): lax.psum_scatter(grad_output.astype(jnp.bfloat16), 'dp', scatter_dimensio...  75 us
    reduce_scatter x1, waiting for transfers between devices, body(): lax.psum_scatter(grad_query.astype(jnp.bfloat16), 'dp', scatter_dimension...  73.7 us
  transfers between devices with their start and end apart: 14, of which 11 were waited for; matrix products, arithmetic and copies ran while one was open for 15% of the time, Pallas kernels for 0%

commit v1 on v0

v1 whole, which is shorter than its diff:
```python
import functools

import jax
import jax.numpy as jnp
from jax import lax
from jax.experimental import pallas as pl
from jax.experimental.pallas import tpu as pltpu
from jax.sharding import PartitionSpec as P

HEADS = 16
HD = 128
HIST = 8
STREAMS = 4
MIXH = 32
MIXOUT = 36
F32 = jnp.float32
BF16 = jnp.bfloat16

ORDER = (0, 2, 4, 6, 1, 3, 5, 7)


def rms_scale(value, gain):
    return value * lax.rsqrt(jnp.mean(value * value, axis=-1, keepdims=True) + 1e-06) * gain


def rotary(heads_value):
    row_count = heads_value.shape[0]
    half_size = heads_value.shape[-1] // 2
    freqs = 10000.0 ** (-jnp.arange(half_size, dtype=jnp.float32) / half_size)
    angles = jnp.arange(row_count, dtype=jnp.float32)[:, None] * freqs[None, :]
    cos_part = jnp.cos(angles)[:, None, :]
    sin_part = jnp.sin(angles)[:, None, :]
    first_half = heads_value[..., :half_size]
    second_half = heads_value[..., half_size:]
    return jnp.concatenate(
        [
            first_half * cos_part - second_half * sin_part,
            second_half * cos_part + first_half * sin_part,
        ],
        axis=-1,
    )


def norm_back(value, gain, grad_normed):
    unused, pullback = jax.vjp(rms_scale, value, gain)
    return pullback(grad_normed)


def gelu_back(value, grad_value):
    unused, pullback = jax.vjp(jax.nn.gelu, value)
    return pullback(grad_value)[0]


def rotary_back(value, grad_value):
    unused, pullback = jax.vjp(rotary, value)
    return pullback(grad_value)[0]


def after(value, *earlier):
    return lax.optimization_barrier((value,) + earlier)[0]


class Group:
    def __init__(self, count, rep):
        self.count = count
        self.rep = rep
        self.fast = count == 8
        self.me = lax.axis_index("dp")
        self.chain = [None, None, None]

    def swap(self, value, k):
        return lax.ppermute(value, "dp", [(i, i ^ k) for i in range(self.count)])

    def blocks(self, value, axis):
        if not self.fast:
            return value
        size = value.shape[axis] // self.count
        return jnp.concatenate(
            [lax.dynamic_slice_in_dim(value, (self.me ^ k) * size, size, axis) for k in ORDER], axis
        )

    def natural(self, value, axis):
        if not self.fast:
            return value
        size = value.shape[axis] // self.count
        where = jnp.array([ORDER.index(k) for k in range(self.count)], jnp.int32)
        return jnp.concatenate(
            [
                lax.dynamic_slice_in_dim(value, where[self.me ^ j] * size, size, axis)
                for j in range(self.count)
            ],
            axis,
        )

    def gather_start(self, piece, between=()):
        axis = piece.ndim - 2
        half = piece.shape[axis] // 2
        from_x = self.swap(piece, 2)
        from_y = self.swap(piece, 4)
        if between:
            from_x, from_y = after(from_x, *between), after(from_y, *between)
        far_a = self.swap(from_y[..., :half, :], 2)
        far_b = self.swap(from_x[..., half:, :], 4)
        near = jnp.concatenate([piece, from_x, from_y], axis)
        return near, jnp.concatenate([far_a, far_b], axis), self.swap(near, 1)

    def gather(self, piece):
        if not self.fast:
            return lax.all_gather(piece, "dp", axis=0, tiled=True)
        near, far, other = self.gather_start(piece)
        return jnp.concatenate([near, far, other, self.swap(far, 1)], 0)

    def scatter_sum(self, same, other, earlier=()):
        if not self.fast:
            whole = jnp.concatenate([same, other], 0)
            return lax.psum_scatter(whole, "dp", scatter_dimension=0, tiled=True).astype(F32), ()
        rows = same.shape[0] // 4
        half = rows // 2
        chip = (same.astype(F32) + self.swap(other, 1).astype(F32)).astype(BF16)
        to_x = jnp.concatenate([chip[rows : rows + half], chip[3 * rows : 3 * rows + half]], 0)
        to_y = jnp.concatenate([chip[2 * rows + half : 3 * rows], chip[3 * rows + half :]], 0)
        if earlier:
            to_x, to_y = after(to_x, *earlier), after(to_y, *earlier)
        from_x = self.swap(to_x, 2)
        from_y = self.swap(to_y, 4)
        seen = (from_x, from_y)
        from_x, from_y = from_x.astype(F32), from_y.astype(F32)
        pass_y = (chip[2 * rows : 2 * rows + half].astype(F32) + from_x[half:]).astype(BF16)
        pass_x = (chip[rows + half : 2 * rows].astype(F32) + from_y[half:]).astype(BF16)
        own_a = chip[:half].astype(F32) + from_x[:half] + self.swap(pass_y, 4).astype(F32)
        own_b = chip[half:rows].astype(F32) + from_y[:half] + self.swap(pass_x, 2).astype(F32)
        return jnp.concatenate([own_a, own_b], 0), seen

    def gather_small(self, value):
        if not self.fast:
            return lax.all_gather(value, "dp", axis=0, tiled=False)
        value = value[None]
        for k in (1, 2, 4):
            value = jnp.concatenate([value, self.swap(value, k)], 0)
        return jnp.concatenate(
            [lax.dynamic_slice_in_dim(value, self.me ^ j, 1, 0) for j in range(self.count)], 0
        )

    def sum_all(self, value):
        if not self.fast or self.rep != 4:
            return lax.psum(value, ("rep", "dp"))
        for k in (1, 2, 4):
            value = value + self.swap(value, k)
        for k in (1, 2):
            value = value + lax.ppermute(value, "rep", [(i, i ^ k) for i in range(self.rep)])
        return value

    def exchange_columns(self, value):
        if not self.fast:
            return lax.all_to_all(value, "dp", split_axis=1, concat_axis=0, tiled=True)
        size = value.shape[1] // self.count
        pieces = []
        for k in ORDER:
            piece = lax.dynamic_slice_in_dim(value, (self.me ^ k) * size, size, 1)
            pieces.append(self.swap(piece, k) if k else piece)
        return self.natural(jnp.concatenate(pieces, 0), 0)

    def exchange_rows(self, value):
        size = value.shape[0] // self.count
        if not self.fast:
            whole = lax.all_to_all(value, "dp", split_axis=0, concat_axis=1, tiled=True)
            return jnp.split(whole, self.count, axis=1)
        pieces = []
        for k in ORDER:
            piece = lax.dynamic_slice_in_dim(value, (self.me ^ k) * size, size, 0)
            pieces.append(self.swap(piece, k) if k else piece)
        return pieces

    def link(self, value, stage, pairs):
        if self.chain[stage] is not None:
            value = after(value, self.chain[stage])
        moved = lax.ppermute(value, "rep", pairs)
        self.chain[stage] = moved
        return moved

    def rep_sum(self, value):
        if self.rep != 4:
            return lax.psum(value, "rep").astype(F32)
        place = lax.axis_index("rep")
        first = self.link(value, 0, [(0, 1), (3, 2)])
        half = lax.reduce_precision(value.astype(F32) + first.astype(F32), 8, 7)
        across = self.link(half.astype(BF16), 1, [(1, 2), (2, 1)])
        total = lax.reduce_precision(half + across.astype(F32), 8, 7)
        last = self.link(total.astype(BF16), 2, [(1, 0), (2, 3)])
        return jnp.where((place == 0) | (place == 3), last.astype(F32), total)


def forward_dot(value, pieces):
    block = value.shape[1] // 8
    starts, sizes = (0, 3, 4, 7), (3, 1, 3, 1)
    total = 0.0
    for piece, start, size in zip(pieces, starts, sizes):
        if piece is not None:
            part = value[:, start * block : (start + size) * block]
            total = total + jnp.dot(part, piece, preferred_element_type=F32)
    return total


def backward_dot(value, pieces):
    return jnp.concatenate(
        [jnp.einsum("te,de->td", value, piece, preferred_element_type=F32) for piece in pieces], 1
    )


def mix_block(mix, index):
    return mix[:, index : index + 1]


def streams_kernel(block, order, me_ref, history_ref, mix_ref, gain_ref, streams_ref, q_ref, k_ref, v_ref):
    mix = mix_ref[...]
    width = streams_ref.shape[2]
    squares = [0.0, 0.0, 0.0]
    for start in range(0, width, block):
        at = pl.ds(start, block)
        sums = [None] * STREAMS
        for j in range(HIST):
            past = history_ref[j, :, at].astype(F32)
            for s in range(STREAMS):
                term = mix_block(mix, s * HIST + j) * past
                sums[s] = term if sums[s] is None else sums[s] + term
        for s in range(STREAMS):
            streams_ref[s, :, at] = sums[s]
            if s < 3:
                squares[s] = squares[s] + jnp.sum(sums[s] * sums[s], axis=1, keepdims=True)
    scales = [lax.rsqrt(total / width + 1e-06) for total in squares]
    for s, out_ref in enumerate((q_ref, k_ref, v_ref)):
        for place, k in enumerate(order):
            at = pl.ds(pl.multiple_of((me_ref[0] ^ k) * block, block), block)
            normed = streams_ref[s, :, at] * scales[s] * gain_ref[s : s + 1, at]
            out_ref[:, place * block : (place + 1) * block] = normed.astype(BF16)


def mixed_streams(me, order, history, stream_mix, gains):
    hist, rows, width = history.shape
    tile = 32
    token = pl.BlockSpec((tile, width), lambda i, me: (i, 0))
    out = jax.ShapeDtypeStruct((rows, width), BF16)
    return pl.pallas_call(
        functools.partial(streams_kernel, width // len(order), order),
        grid_spec=pltpu.PrefetchScalarGridSpec(
            num_scalar_prefetch=1,
            grid=(rows // tile,),
            in_specs=[
                pl.BlockSpec((hist, tile, width), lambda i, me: (0, i, 0)),
                pl.BlockSpec((tile, STREAMS * HIST), lambda i, me: (i, 0)),
                pl.BlockSpec((3, width), lambda i, me: (0, 0)),
            ],
            out_specs=[
                pl.BlockSpec((STREAMS, tile, width), lambda i, me: (0, i, 0)),
                token,
                token,
                token,
            ],
        ),
        out_shape=[jax.ShapeDtypeStruct((STREAMS, rows, width), F32), out, out, out],
        cost_estimate=pl.CostEstimate(
            flops=2 * STREAMS * HIST * rows * width,
            bytes_accessed=rows * width * (2 * hist + 4 * STREAMS + 6),
            transcendentals=0,
        ),
        compiler_params=pltpu.CompilerParams(vmem_limit_bytes=32 * 1024 * 1024),
        name="streams",
    )(me, history, stream_mix, gains)


def streams_back_kernel(
    block, order, me_ref, history_ref, mix_ref, gain_ref, streams_ref, q_ref, k_ref, v_ref, rest_ref,
    history_out, mix_out, gain_out, sums_ref, gain_sums,
):
    mix = mix_ref[...]
    rows, width = rest_ref.shape
    grads = (q_ref, k_ref, v_ref)
    scales, shifts = [], []
    for s in range(3):
        squares, cross = 0.0, 0.0
        for place, k in enumerate(order):
            at = pl.ds(pl.multiple_of((me_ref[0] ^ k) * block, block), block)
            value = streams_ref[s, :, at]
            grad = grads[s][:, place * block : (place + 1) * block] * gain_ref[s : s + 1, at]
            squares = squares + jnp.sum(value * value, axis=1, keepdims=True)
            cross = cross + jnp.sum(value * grad, axis=1, keepdims=True)
        scale = lax.rsqrt(squares / width + 1e-06)
        scales.append(scale)
        shifts.append(scale * scale * scale * (cross / width))
    sums_ref[...] = jnp.zeros_like(sums_ref)

    @pl.when(pl.program_id(0) == 0)
    def _():
        gain_sums[...] = jnp.zeros_like(gain_sums)

    for place, k in enumerate(order):
        for part in range(0, block, 128):
            lane = place * block + part
            at = pl.ds(pl.multiple_of((me_ref[0] ^ k) * block + part, 128), 128)
            backs = []
            for s in range(3):
                value = streams_ref[s, :, at]
                raw = grads[s][:, lane : lane + 128]
                grad = raw * gain_ref[s : s + 1, at]
                over = (raw * value * scales[s]).reshape(rows // 8, 8, 128)
                gain_sums[s, :, at] += jnp.sum(over, axis=0)
                backs.append(grad * scales[s] - value * shifts[s])
            backs.append(rest_ref[:, at])
            for j in range(HIST):
                past = history_ref[j, :, at].astype(F32)
                total = None
                for s in range(STREAMS):
                    term = mix_block(mix, s * HIST + j) * backs[s]
                    total = term if total is None else total + term
                    sums_ref[s * HIST + j] += backs[s] * past
                history_out[j, :, at] = total.astype(BF16)
    for index in range(STREAMS * HIST):
        mix_out[:, index : index + 1] = jnp.sum(sums_ref[index], axis=1, keepdims=True)

    @pl.when(pl.program_id(0) == pl.num_programs(0) - 1)
    def _():
        gain_out[...] = jnp.sum(gain_sums[...], axis=1)


def streams_back(me, order, history, stream_mix, gains, streams, d_q, d_k, d_v, d_rest):
    hist, rows, width = history.shape
    tile = 32
    token = pl.BlockSpec((tile, width), lambda i, me: (i, 0))
    stored = pl.BlockSpec((hist, tile, width), lambda i, me: (0, i, 0))
    weight = pl.BlockSpec((tile, STREAMS * HIST), lambda i, me: (i, 0))
    return pl.pallas_call(
        functools.partial(streams_back_kernel, width // len(order), order),
        grid_spec=pltpu.PrefetchScalarGridSpec(
            num_scalar_prefetch=1,
            grid=(rows // tile,),
            in_specs=[
                stored,
                weight,
                pl.BlockSpec((3, width), lambda i, me: (0, 0)),
                pl.BlockSpec((3, tile, width), lambda i, me: (0, i, 0)),
                token,
                token,
                token,
                token,
            ],
            out_specs=[stored, weight, pl.BlockSpec((3, width), lambda i, me: (0, 0))],
            scratch_shapes=[
                pltpu.VMEM((STREAMS * HIST, tile, 128), F32),
                pltpu.VMEM((3, 8, width), F32),
            ],
        ),
        out_shape=[
            jax.ShapeDtypeStruct(history.shape, BF16),
            jax.ShapeDtypeStruct((rows, STREAMS * HIST), F32),
            jax.ShapeDtypeStruct((3, width), F32),
        ],
        cost_estimate=pl.CostEstimate(
            flops=4 * STREAMS * HIST * rows * width,
            bytes_accessed=rows * width * (4 * hist + 28),
            transcendentals=0,
        ),
        compiler_params=pltpu.CompilerParams(vmem_limit_bytes=32 * 1024 * 1024),
        name="streams_back",
    )(me, history, stream_mix, gains, streams, d_q, d_k, d_v, d_rest)


def body(
    rep,
    count,
    history,
    stream_mix,
    lengths,
    w_query,
    w_key,
    w_value,
    w_output,
    gain_query,
    gain_key,
    gain_value,
    w_up,
    w_down,
    gain_mlp,
    w_mix_in,
    w_mix_out,
    gain_mix,
    grad_block,
    grad_next,
):
    group = Group(count, rep)
    me = group.me
    row_count = history.shape[1]
    width = history.shape[2]
    shard = width // count
    valid_count = lengths[0]
    position = jnp.arange(row_count, dtype=jnp.int32)
    row_keep = (position < valid_count).astype(F32)[:, None]
    score_scale = HD ** (-0.5)

    out_shard = w_mix_out.reshape(-1)
    out_row = jnp.zeros((shard,), BF16).at[: out_shard.shape[0]].set(out_shard)
    small = jnp.concatenate(
        [
            jnp.stack([gain_query, gain_key, gain_value, gain_mlp, gain_mix, out_row]),
            w_mix_in.T,
        ],
        0,
    )
    small = group.gather_small(small)
    gains = small[:, :5].transpose(1, 0, 2).reshape(5, width).astype(F32)
    full_gain_q, full_gain_k, full_gain_v, full_gain_m, full_gain_x = (gains[i] for i in range(5))
    full_mix_out = small[:, 5, : out_shard.shape[0]].reshape(MIXH, MIXOUT)
    full_mix_in = small[:, 6:].transpose(1, 0, 2).reshape(MIXH, width)

    order = ORDER if group.fast else tuple(range(8))
    place = (me if group.fast else jnp.zeros_like(me)).astype(jnp.int32)[None]
    streams, normed_q, normed_k, normed_v = mixed_streams(
        place, order, history, stream_mix, gains[:3]
    )
    three = jnp.stack([w_query, w_key, w_value])
    normed = (normed_q, normed_k, normed_v)
    if group.fast:
        near, far, near_other = group.gather_start(three, (normed_q,))
        early = [
            forward_dot(normed[i], (near[i], None, near_other[i], None)) for i in range(3)
        ]
        far_other = group.swap(after(far, *early), 1)
        query, keys, values = (
            early[i] + forward_dot(normed[i], (None, far[i], None, far_other[i])) for i in range(3)
        )
        full_query, full_key, full_value = (
            (near[i], far[i], near_other[i], far_other[i]) for i in range(3)
        )
        w_output, w_up = after(w_output, far), after(w_up, far)
    else:
        three = lax.all_gather(three, "dp", axis=1, tiled=True)
        query, keys, values = (
            jnp.dot(normed[i], three[i], preferred_element_type=F32) for i in range(3)
        )
        full_query, full_key, full_value = ((three[i],) for i in range(3))
    full_output = lax.all_gather(w_output, "dp", axis=0, tiled=True)
    up_cols = group.exchange_columns(w_up)
    query = query.reshape(row_count, HEADS, HD)
    keys = keys.reshape(row_count, HEADS, HD)
    value_heads = values.astype(BF16).reshape(row_count, HEADS, HD)
    query_rot = rotary(query).astype(BF16)
    keys_rot = rotary(keys).astype(BF16)
    raw_scores = (
        jnp.einsum("qhe,khe->hqk", query_rot, keys_rot, preferred_element_type=F32) * score_scale
    )
    allowed = (position[None, :] <= position[:, None]) & (position[None, :] < valid_count)
    scores = jnp.where(allowed[None], raw_scores, -1e30)
    row_max = jnp.max(scores, axis=-1, keepdims=True)
    weights = jnp.exp(scores - row_max)
    probs = weights / jnp.sum(weights, axis=-1, keepdims=True)
    probs_low = probs.astype(BF16)
    mixed = (
        jnp.einsum("hqk,khe->qhe", probs_low, value_heads, preferred_element_type=F32)
        .astype(BF16)
        .reshape(row_count, HEADS * HD)
    )
    hidden = streams[3] + jnp.dot(mixed, full_output, preferred_element_type=F32)

    normed_m = rms_scale(hidden, full_gain_m).astype(BF16)
    normed_all = group.gather(normed_m)
    middle = normed_all.shape[0] // 2
    upper = jnp.dot(normed_all, up_cols, preferred_element_type=F32)
    active, slope = jax.vjp(jax.nn.gelu, upper)
    slope = slope(jnp.ones_like(upper))[0]
    active, slope = lax.optimization_barrier((active.astype(BF16), slope))
    part_other = jnp.dot(active[middle:], w_down, preferred_element_type=F32).astype(BF16)
    part_same = jnp.dot(active[:middle], w_down, preferred_element_type=F32).astype(BF16)
    block = hidden + group.scatter_sum(part_same, part_other)[0]

    normed_x = rms_scale(block, full_gain_x).astype(BF16)
    inner = jnp.einsum("td,kd->tk", normed_x, full_mix_in, preferred_element_type=F32)
    inner_act = jax.nn.gelu(inner).astype(BF16)
    logits = jnp.dot(inner_act, full_mix_out, preferred_element_type=F32)
    block_output = (block * row_keep).astype(BF16)
    next_mix = logits * row_keep
    d_logits = (grad_next * row_keep).astype(BF16)
    grad_mix_out = jnp.einsum("tk,to->ko", inner_act, d_logits, preferred_element_type=F32)
    d_inner_act = jnp.einsum("to,ko->tk", d_logits, full_mix_out, preferred_element_type=F32)
    d_inner = gelu_back(inner, d_inner_act).astype(BF16)
    grad_mix_in = jnp.einsum("tk,td->kd", d_inner, normed_x, preferred_element_type=F32)
    d_normed_x = jnp.dot(d_inner, full_mix_in, preferred_element_type=F32)
    d_block_norm, grad_gain_x = norm_back(block, full_gain_x, d_normed_x)
    d_block = grad_block.astype(F32) * row_keep + d_block_norm

    d_block_low = d_block.astype(BF16)
    d_block_all = group.gather(d_block_low)
    grad_down = jnp.einsum("tf,td->fd", active, d_block_all, preferred_element_type=F32)
    grad_down = grad_down.astype(BF16)
    d_active = jnp.einsum(
        "td,fd->tf", after(d_block_all, grad_down), w_down, preferred_element_type=F32
    )
    d_upper = (slope * d_active).astype(BF16)
    back_other = jnp.einsum("tf,df->td", d_upper[middle:], up_cols, preferred_element_type=F32)
    back_same = jnp.einsum("tf,df->td", d_upper[:middle], up_cols, preferred_element_type=F32)
    back_same, back_other = back_same.astype(BF16), back_other.astype(BF16)
    d_normed_m, seen = group.scatter_sum(back_same, back_other)
    grad_up = jnp.einsum(
        "td,tf->df", after(normed_all, back_same), d_upper, preferred_element_type=F32
    ).astype(BF16)
    up_pieces = group.exchange_rows(after(grad_up, *seen) if seen else grad_up)
    d_hidden_norm, grad_gain_m = norm_back(hidden, full_gain_m, d_normed_m)
    d_hidden = d_block + d_hidden_norm

    d_hidden_low = d_hidden.astype(BF16)

    half_width = width // 2

    def weight_grad(inputs, outputs, earlier):
        def rows(columns):
            return jnp.einsum("td,te->de", columns, outputs, preferred_element_type=F32).astype(BF16)

        other = rows(inputs[:, half_width:])
        same = rows(inputs[:, :half_width])
        own, seen = group.scatter_sum(same, other, earlier)
        return own.astype(BF16), seen

    part_output, seen = weight_grad(group.blocks(mixed, 1), d_hidden_low, ())
    d_mixed = jnp.einsum("te,de->td", d_hidden_low, full_output, preferred_element_type=F32)
    d_mixed = d_mixed.astype(BF16).reshape(row_count, HEADS, HD)
    d_probs = jnp.einsum("qhe,khe->hqk", d_mixed, value_heads, preferred_element_type=F32)
    d_values = jnp.einsum("hqk,qhe->khe", probs_low, d_mixed, preferred_element_type=F32)
    row_delta = jnp.sum(probs * d_probs, axis=-1, keepdims=True)
    d_scores = (probs * (d_probs - row_delta)).astype(BF16)
    d_query_rot = (
        jnp.einsum("hqk,khe->qhe", d_scores, keys_rot, preferred_element_type=F32) * score_scale
    )
    d_keys_rot = (
        jnp.einsum("hqk,qhe->khe", d_scores, query_rot, preferred_element_type=F32) * score_scale
    )
    d_query = rotary_back(query, d_query_rot).astype(BF16).reshape(row_count, HEADS * HD)
    d_keys = rotary_back(keys, d_keys_rot).astype(BF16).reshape(row_count, HEADS * HD)
    d_values = d_values.astype(BF16).reshape(row_count, HEADS * HD)
    part_value, seen = weight_grad(normed_v, d_values, seen)
    part_query, seen = weight_grad(normed_q, d_query, seen)
    part_key, seen = weight_grad(normed_k, d_keys, seen)
    out_down = lax.psum(grad_down, "rep")
    per = count // 2
    up_sums = [group.rep_sum(jnp.concatenate(up_pieces[i : i + per], 1)) for i in (0, per)]
    out_up = group.natural(jnp.concatenate(up_sums, 1), 1)
    grad_output, grad_value = jnp.split(
        lax.psum(after(jnp.concatenate([part_output, part_value], 0), out_down), "rep"), 2
    )
    grad_query = group.rep_sum(part_query)
    grad_key = group.rep_sum(part_key)
    out_down = after(out_down, part_key)

    grad_history, grad_stream_mix, grad_gains = streams_back(
        place,
        order,
        history,
        stream_mix,
        gains[:3],
        streams,
        backward_dot(d_query, full_query),
        backward_dot(d_keys, full_key),
        backward_dot(d_values, full_value),
        d_hidden,
    )

    flat_out = grad_mix_out.reshape(-1)
    out_grad_row = jnp.zeros((width,), F32).at[: flat_out.shape[0]].set(flat_out)
    early = jnp.concatenate(
        [jnp.stack([grad_gain_x, grad_gain_m, out_grad_row]), grad_mix_in], 0
    )
    early = group.sum_all(early)
    late = group.sum_all(grad_gains)
    own_early = lax.dynamic_slice_in_dim(early, me * shard, shard, 1)
    own_late = lax.dynamic_slice_in_dim(late, me * shard, shard, 1)
    rows_out = MIXH // count
    own_mix_out = lax.dynamic_slice_in_dim(early[2], me * rows_out * MIXOUT, rows_out * MIXOUT, 0)

    return (
        block_output,
        next_mix,
        grad_history,
        grad_stream_mix,
        grad_query,
        grad_key,
        grad_value.astype(F32),
        grad_output.astype(F32),
        own_late[0],
        own_late[1],
        own_late[2],
        out_up,
        out_down.astype(F32),
        own_early[1],
        own_early[3:].T,
        own_mix_out.reshape(rows_out, MIXOUT),
        own_early[0],
    )


def solution(mesh):
    rep, count = mesh.shape["rep"], mesh.shape["dp"]

    def step(*args):
        return body(rep, count, *args)

    return jax.shard_map(
        step,
        mesh=mesh,
        in_specs=(
            P(None, ("rep", "dp"), None),
            P(("rep", "dp"), None),
            P(("rep", "dp")),
            P("dp", None),
            P("dp", None),
            P("dp", None),
            P("dp", None),
            P("dp"),
            P("dp"),
            P("dp"),
            P("dp", None),
            P("dp", None),
            P("dp"),
            P("dp", None),
            P("dp", None),
            P("dp"),
            P(("rep", "dp"), None),
            P(("rep", "dp"), None),
        ),
        out_specs=(
            P(("rep", "dp"), None),
            P(("rep", "dp"), None),
            P(None, ("rep", "dp"), None),
            P(("rep", "dp"), None),
            P("dp", None),
            P("dp", None),
            P("dp", None),
            P("dp", None),
            P("dp"),
            P("dp"),
            P("dp"),
            P("dp", None),
            P("dp", None),
            P("dp"),
            P("dp", None),
            P("dp", None),
            P("dp"),
        ),
        check_vma=False,
    )
```

time: 1870 us -> 1120 us (0.60)
  waiting for transfers between devices: 1330 us -> 567 us
  blocking collectives: 112 us -> 0 us
  starting transfers between devices: 1.14 us -> 103 us
  matrix products: 286 us -> 189 us
  other arithmetic: 52.1 us -> 116 us
  Pallas kernels: 0 us -> 31.4 us
    reduce_scatter x7 -> x0, waiting for transfers between devices: 642 us -> none  [the longest x1 209 us: body(): lax.psum_scatter(grad_up.astype(jnp.bfloat16), 'dp', scatter_dimension=0,...]
    ppermute x0 -> x87, waiting for transfers between devices: none -> 562 us  [the longest x71 412 us: swap(): return lax.ppermute(value, 'dp', [(i, i ^ k) for i in range(self.count)])]
    all_gather x6 -> x1, waiting for transfers between devices: 373 us -> 5.69 us  [body(): full_output = lax.all_gather(w_output, 'dp', axis=0, tiled=True)]
    psum x1 -> x2, waiting for transfers between devices: 314 us -> 0.02 us  [the longest x1 0.02 us: body(): lax.psum(after(jnp.concatenate([part_output, part_value], 0), out_down),...]
    dot_general x32 -> x52, matrix products: 284 us -> 180 us  [the longest x12 29.3 us: backward_dot(): jnp.einsum('te,de->td', value, piece, preferred_element_type=F32)]
    ppermute x0 -> x87, starting transfers between devices: none -> 103 us  [the longest x71 60.8 us: swap(): return lax.ppermute(value, 'dp', [(i, i ^ k) for i in range(self.count)])]
    all_gather x7 -> x0, blocking collectives: 62.7 us -> none  [the longest x1 10.3 us: body(): lax.all_gather(gain_mix, 'dp', axis=0, tiled=True)]
    pallas_call x0 -> x2, Pallas kernels: none -> 31.4 us  [the longest x1 23.4 us: streams_back(): pl.pallas_call(functools.partial(streams_back_kernel, width // len(order)...]
  transfers between devices with their start and end apart: 14 -> 90, of which waited for: 11 -> 50; matrix products, arithmetic and copies ran while one was open for 15% -> 24% of each run, Pallas kernels for 0% -> 3%
where the time goes in v1:
time: 1120 us; the launch traced here: 1110 us
  waiting for transfers between devices  567 us (51%)
  matrix products  189 us (17%)
  other arithmetic  116 us (10%)
  starting transfers between devices  103 us (9%)
  local copies, waits for them, and re-layouts  76.3 us (7%)
  Pallas kernels  31.4 us (3%)
  between operations  27.8 us (2%)
    ppermute x71, waiting for transfers between devices, swap(): return lax.ppermute(value, 'dp', [(i, i ^ k) for i in range(self.count)])  412 us
    ppermute x12, waiting for transfers between devices, link(): moved = lax.ppermute(value, 'rep', pairs)  101 us
    ppermute x71, starting transfers between devices, swap(): return lax.ppermute(value, 'dp', [(i, i ^ k) for i in range(self.count)])  60.8 us
    ppermute x4, waiting for transfers between devices, sum_all(): lax.ppermute(value, 'rep', [(i, i ^ k) for i in range(self.rep)])  48.5 us
    unnamed x293, local copies, waits for them, and re-layouts  44.8 us
    dot_general x12, matrix products, backward_dot(): jnp.einsum('te,de->td', value, piece, preferred_element_type=F32)  29.3 us
    ppermute x12, starting transfers between devices, link(): moved = lax.ppermute(value, 'rep', pairs)  29.2 us
    dot_general x12, matrix products, forward_dot(): total = total + jnp.dot(part, piece, preferred_element_type=F32)  26.1 us
  transfers between devices with their start and end apart: 90, of which 50 were waited for; matrix products, arithmetic and copies ran while one was open for 24% of the time, Pallas kernels for 3%

profile of v1, /device:TPU:0, one launch (start us, length us, event | category | flops | bytes accessed | tf_op | source)
XLA Modules:
  0.0 1111.6 jit_solution(17564263582998891745)
XLA Ops:
  7.3 3.9 pad_maximum_fusion.1
  17.9 67.0 %collective-permute-done.1 = bf16[2,38,256]{2,1,0:T(8,128)(2,1)S(1)} collective-permute-done((bf16[2,38,256]{2,1,0:T(8,128)(2,1)S(1)}, bf16[2,38,256]{2,1,0:T(8,128)(2,1)S(1)}, u32[]{:S(2)}, u32[]{:S(2)}) %collective-permute-start.1) | collective-permute-done | bytes 38944 | tf_op jit(solution)/shard_map/ppermute | solution.py:72
  85.3 4.0 collective-permute-done.2
  93.0 8.0 streams.1
  101.1 9.4 pad_maximum_fusion
  115.7 33.2 %collective-permute-done.6 = bf16[3,128,2048]{2,1,0:T(8,128)(2,1)S(1)} collective-permute-done((bf16[3,128,2048]{2,1,0:T(8,128)(2,1)S(1)}, bf16[3,128,2048]{2,1,0:T(8,128)(2,1)S(1)}, u32[]{:S(2)}, u32[]{:S(2)}) %collective-permute-start.6) | collective-permute-done | bytes 1572896 | tf_op jit(solution)/shard_map/ppermute | solution.py:72
  173.1 3.9 collective-permute-done.8
  187.6 4.1 subtract_convert_fusion.1
  191.6 6.4 fusion.184
  201.2 5.7 all-gather.2.cloned.1.call-done
  206.9 6.4 multiply_reduce_fusion.6
  217.3 4.0 constant_dynamic-slice_fusion.20
  224.9 17.1 %collective-permute-done.10 = bf16[256,2048]{1,0:T(8,128)(2,1)S(1)} collective-permute-done((bf16[256,2048]{1,0:T(8,128)(2,1)}, bf16[256,2048]{1,0:T(8,128)(2,1)S(1)}, u32[]{:S(2)}, u32[]{:S(2)}) %collective-permute-start.10) | collective-permute-done | bytes 1048608 | tf_op jit(solution)/shard_map/ppermute | solution.py:72
  245.8 8.6 collective-permute-done.17
  260.2 5.1 collective-permute-done.15
  276.8 13.5 %collective-permute-done.20 = bf16[256,1024]{1,0:T(8,128)(2,1)S(1)} collective-permute-done((bf16[256,1024]{1,0:T(8,128)(2,1)}, bf16[256,1024]{1,0:T(8,128)(2,1)S(1)}, u32[]{:S(2)}, u32[]{:S(2)}) %collective-permute-start.20) | collective-permute-done | bytes 524320 | tf_op jit(solution)/shard_map/ppermute | solution.py:72
  299.3 10.2 collective-permute-done.11
  316.1 15.3 %fusion.6 = (f32[2048,1024]{1,0:T(8,128)}, bf16[2048,1024]{1,0:T(8,128)(2,1)S(1)}) fusion(bf16[2048,2048]{1,0:T(8,128)(2,1)S(1)} %constant_dynamic-update-slice_fusion.10, bf16[2048,1024]{1,0:T(8,128)(2,1)S(1)} %dynamic-slice_dynamic-update-slice_fusion), kind=kOutput, calls=%fused_computation.25 | convolution fusion | flops 8629780480 | bytes 25165824 | tf_op jit(solution)/shard_map/dot_general | solution.py:466
  333.4 4.7 convolution_convert_fusion.7
  338.7 6.8 collective-permute-done.22
  345.5 6.5 add_convert_fusion.5
  353.9 23.8 %collective-permute-done.23 = bf16[256,2048]{1,0:T(8,128)(2,1)S(1)} collective-permute-done((bf16[256,2048]{1,0:T(8,128)(2,1)S(1)}, bf16[256,2048]{1,0:T(8,128)(2,1)S(1)}, u32[]{:S(2)}, u32[]{:S(2)}) %collective-permute-start.23) | collective-permute-done | bytes 1048608 | tf_op jit(solution)/shard_map/ppermute | solution.py:72
  378.7 12.9 %collective-permute-done.24 = bf16[128,2048]{1,0:T(8,128)(2,1)S(1)} collective-permute-done((bf16[128,2048]{1,0:T(8,128)(2,1)S(1)}, bf16[128,2048]{1,0:T(8,128)(2,1)S(1)}, u32[]{:S(2)}, u32[]{:S(2)}) %collective-permute-start.24) | collective-permute-done | bytes 524320 | tf_op jit(solution)/shard_map/ppermute | solution.py:72
  393.3 12.3 %collective-permute-done.26 = bf16[128,2048]{1,0:T(8,128)(2,1)} collective-permute-done((bf16[128,2048]{1,0:T(8,128)(2,1)}, bf16[128,2048]{1,0:T(8,128)(2,1)}, u32[]{:S(2)}, u32[]{:S(2)}) %collective-permute-start.26) | collective-permute-done | bytes 524320 | tf_op jit(solution)/shard_map/ppermute | solution.py:72
  413.9 21.4 %collective-permute-done.28 = bf16[256,2048]{1,0:T(8,128)(2,1)S(1)} collective-permute-done((bf16[256,2048]{1,0:T(8,128)(2,1)S(1)}, bf16[256,2048]{1,0:T(8,128)(2,1)S(1)}, u32[]{:S(2)}, u32[]{:S(2)}) %collective-permute-start.28) | collective-permute-done | bytes 1048608 | tf_op jit(solution)/shard_map/ppermute | solution.py:72
  438.0 12.1 %collective-permute-done.29 = bf16[128,2048]{1,0:T(8,128)(2,1)S(1)} collective-permute-done((bf16[128,2048]{1,0:T(8,128)(2,1)S(1)}, bf16[128,2048]{1,0:T(8,128)(2,1)S(1)}, u32[]{:S(2)}, u32[]{:S(2)}) %collective-permute-start.29) | collective-permute-done | bytes 524320 | tf_op jit(solution)/shard_map/ppermute | solution.py:72
  457.4 11.0 convolution_convert_fusion.4
  468.4 14.8 %multiply_convert_fusion = bf16[2048,1024]{1,0:T(8,128)(2,1)S(1)} fusion(f32[2048,1024]{1,0:T(8,128)} %get-tuple-element.85, bf16[2048,2048]{1,0:T(8,128)(2,1)} %copy-done.92, bf16[1024,2048]{1,0:T(8,128)(2,1)} %param.35), kind=kOutput, calls=%fused_computation.31 | convolution fusion | flops 8594128896 | bytes 25165824 | tf_op jit(solution)/shard_map/td,fd->tf/dot_general | solution.py:493
  483.2 6.3 convolution_convert_fusion.5
  494.9 7.4 convolution_convert_fusion.6
  502.3 4.1 add_convert_fusion.4
  516.7 18.1 %collective-permute-done.34 = bf16[256,2048]{1,0:T(8,128)(2,1)} collective-permute-done((bf16[256,2048]{1,0:T(8,128)(2,1)}, bf16[256,2048]{1,0:T(8,128)(2,1)}, u32[]{:S(2)}, u32[]{:S(2)}) %collective-permute-start.34) | collective-permute-done | bytes 1048608 | tf_op jit(solution)/shard_map/ppermute | solution.py:72
  537.4 13.1 %convolution_convert_fusion.8 = bf16[2048,1024]{1,0:T(8,128)(2,1)S(1)} fusion(bf16[2048,2048]{1,0:T(8,128)(2,1)} %copy-done.91, bf16[2048,1024]{1,0:T(8,128)(2,1)} %copy-done.118), kind=kOutput, calls=%fused_computation.52 | convolution fusion | flops 8592031744 | bytes 16777216 | tf_op jit(solution)/shard_map/td,tf->df/dot_general | solution.py:501
  557.7 10.1 collective-permute-done.55
  567.8 11.3 %collective-permute-done.54 = bf16[256,1024]{1,0:T(8,128)(2,1)S(1)} collective-permute-done((bf16[256,1024]{1,0:T(8,128)(2,1)S(1)}, bf16[256,1024]{1,0:T(8,128)(2,1)S(1)}, u32[]{:S(2)}, u32[]{:S(2)}) %collective-permute-start.54) | collective-permute-done | bytes 524320 | tf_op jit(solution)/shard_map/ppermute | solution.py:72
  579.1 9.6 collective-permute-start.37
  590.3 4.9 collective-permute-start.56
  598.2 12.5 %collective-permute-done.37 = bf16[128,2048]{1,0:T(8,128)(2,1)S(1)} collective-permute-done((bf16[128,2048]{1,0:T(8,128)(2,1)S(1)}, bf16[128,2048]{1,0:T(8,128)(2,1)S(1)}, u32[]{:S(2)}, u32[]{:S(2)}) %collective-permute-start.37) | collective-permute-done | bytes 524320 | tf_op jit(solution)/shard_map/ppermute | solution.py:72
  627.0 4.0 fusion.10
  645.8 4.3 fusion.18
  684.9 23.4 %streams_back.1 = (bf16[8,256,2048]{2,1,0:T(8,128)(2,1)}, f32[256,32]{1,0:T(8,128)S(1)}, f32[3,2048]{1,0:T(4,128)S(1)}) custom-call(s32[1]{0:T(128)} %bitcast.me_ref, bf16[8,256,2048]{2,1,0:T(8,128)(2,1)S(1)} %bitcast.172, f32[256,32]{1,0:T(8,128)S(1)} %copy.62.mix_ref, f32[3,2048]{1,0:T(4,128)S(1)} %bitcast.174, f32[4,256,2048]{2,1,0:T(8,128)} %copy-done.1, ...), custom_call_target="tpu_custom_call" | custom-call | flops 67108864 | bytes 31457280 | tf_op jit(solution)/shard_map/streams_back/pallas_call | solution.py:331
  744.1 34.7 %collective-permute-done.81 = f32[3,2048]{1,0:T(4,128)S(1)} collective-permute-done((f32[3,2048]{1,0:T(4,128)S(1)}, f32[3,2048]{1,0:T(4,128)S(1)}, u32[]{:S(2)}, u32[]{:S(2)}) %collective-permute-start.81) | collective-permute-done | bytes 24608 | tf_op jit(solution)/shard_map/ppermute | solution.py:150
  782.7 12.3 %collective-permute-done.86 = f32[35,2048]{1,0:T(8,128)S(1)} collective-permute-done((f32[35,2048]{1,0:T(8,128)S(1)}, f32[35,2048]{1,0:T(8,128)S(1)}, u32[]{:S(2)}, u32[]{:S(2)}) %collective-permute-start.86) | collective-permute-done | bytes 286752 | tf_op jit(solution)/shard_map/ppermute | solution.py:150
  829.2 10.8 collective-permute-done.41
  846.9 10.0 collective-permute-done.73
  858.4 5.4 fusion.29
  865.5 6.3 collective-permute-done.43
  871.8 6.6 collective-permute-done.44
  880.2 4.3 convert_select_fusion.1
  886.2 8.3 collective-permute-done.75
  896.1 8.3 collective-permute-done.45
  905.6 11.4 %collective-permute-done.47 = bf16[256,2048]{1,0:T(8,128)(2,1)S(1)} collective-permute-done((bf16[256,2048]{1,0:T(8,128)(2,1)S(1)}, bf16[256,2048]{1,0:T(8,128)(2,1)S(1)}, u32[]{:S(2)}, u32[]{:S(2)}) %collective-permute-start.47) | collective-permute-done | bytes 1048608 | tf_op jit(solution)/shard_map/ppermute | solution.py:72
  919.1 9.1 collective-permute-done.46
  932.2 11.2 %collective-permute-done.66 = bf16[256,2048]{1,0:T(8,128)(2,1)} collective-permute-done((bf16[256,2048]{1,0:T(8,128)(2,1)}, bf16[256,2048]{1,0:T(8,128)(2,1)}, u32[]{:S(2)}, u32[]{:S(2)}) %collective-permute-start.66) | collective-permute-done | bytes 1048608 | tf_op jit(solution)/shard_map/ppermute | solution.py:72
  950.7 6.2 collective-permute-start.58
  962.6 4.2 convert_select_fusion
  966.9 6.2 collective-permute-done.69
  974.5 20.3 %collective-permute-done.58 = bf16[256,2048]{1,0:T(8,128)(2,1)S(1)} collective-permute-done((bf16[256,2048]{1,0:T(8,128)(2,1)S(1)}, bf16[256,2048]{1,0:T(8,128)(2,1)S(1)}, u32[]{:S(2)}, u32[]{:S(2)}) %collective-permute-start.58) | collective-permute-done | bytes 1048608 | tf_op jit(solution)/shard_map/ppermute | solution.py:177
  994.8 4.4 collective-permute-start.70
  1001.4 37.0 %collective-permute-done.70 = bf16[256,2048]{1,0:T(8,128)(2,1)S(1)} collective-permute-done((bf16[256,2048]{1,0:T(8,128)(2,1)S(1)}, bf16[256,2048]{1,0:T(8,128)(2,1)S(1)}, u32[]{:S(2)}, u32[]{:S(2)}) %collective-permute-start.70) | collective-permute-done | bytes 1048608 | tf_op jit(solution)/shard_map/ppermute | solution.py:177
  1044.3 4.9 convert_element_type.582
  1051.7 29.4 %collective-permute-done.64 = bf16[256,2048]{1,0:T(8,128)(2,1)S(1)} collective-permute-done((bf16[256,2048]{1,0:T(8,128)(2,1)S(1)}, bf16[256,2048]{1,0:T(8,128)(2,1)S(1)}, u32[]{:S(2)}, u32[]{:S(2)}) %collective-permute-start.64) | collective-permute-done | bytes 1048608 | tf_op jit(solution)/shard_map/ppermute | solution.py:177
  1083.4 4.2 slice_convert_fusion
  1089.6 12.0 %collective-permute-done.72 = bf16[256,2048]{1,0:T(8,128)(2,1)} collective-permute-done((bf16[256,2048]{1,0:T(8,128)(2,1)}, bf16[256,2048]{1,0:T(8,128)(2,1)}, u32[]{:S(2)}, u32[]{:S(2)}) %collective-permute-start.72) | collective-permute-done | bytes 1048608 | tf_op jit(solution)/shard_map/ppermute | solution.py:177
  (630 shorter events, 335.2 us)
Async XLA Ops:
  7.2 199.7 %all-gather.2.cloned.1.call-start = ((), (), s32[]{:S(2)}) async-start(), calls=%async_computation | async-start | bytes 9437184 | tf_op jit(solution)/shard_map/all_gather | solution.py:440
  11.2 89.8 %collective-permute-start.4 = (bf16[3,256,2048]{2,1,0:T(8,128)(2,1)}, bf16[3,256,2048]{2,1,0:T(8,128)(2,1)}, u32[]{:S(2)}, u32[]{:S(2)}) collective-permute-start(bf16[3,256,2048]{2,1,0:T(8,128)(2,1)} %pad_maximum_fusion.1), channel_id=1, source_target_pairs={{0,4},{1,5},{2,6},{3,7},{4,0},{5,1},{6,2},{7,3},{8,12},{9,13},{10,... | collective-permute-start | bytes 9437192 | tf_op jit(solution)/shard_map/ppermute | solution.py:72
  14.2 86.9 %collective-permute-start.3 = (bf16[3,256,2048]{2,1,0:T(8,128)(2,1)}, bf16[3,256,2048]{2,1,0:T(8,128)(2,1)}, u32[]{:S(2)}, u32[]{:S(2)}) collective-permute-start(bf16[3,256,2048]{2,1,0:T(8,128)(2,1)} %pad_maximum_fusion.1), channel_id=1, source_target_pairs={{0,2},{1,3},{2,0},{3,1},{4,6},{5,7},{6,4},{7,5},{8,10},{9,11},{10,... | collective-permute-start | bytes 9437192 | tf_op jit(solution)/shard_map/ppermute | solution.py:72
  17.4 67.5 %collective-permute-start.1 = (bf16[2,38,256]{2,1,0:T(8,128)(2,1)S(1)}, bf16[2,38,256]{2,1,0:T(8,128)(2,1)S(1)}, u32[]{:S(2)}, u32[]{:S(2)}) collective-permute-start(bf16[2,38,256]{2,1,0:T(8,128)(2,1)S(1)} %pad_maximum_fusion.30), channel_id=1, source_target_pairs={{0,2},{1,3},{2,0},{3,1},{4,6},{5,7},{6,4},{7,5},{8,10},{9,11},{10,... | collective-permute-start | bytes 116744 | tf_op jit(solution)/shard_map/ppermute | solution.py:72
  110.5 42.7 %collective-permute-start.5 = (bf16[3,768,2048]{2,1,0:T(8,128)(2,1)}, bf16[3,768,2048]{2,1,0:T(8,128)(2,1)}, u32[]{:S(2)}, u32[]{:S(2)}) collective-permute-start(bf16[3,768,2048]{2,1,0:T(8,128)(2,1)} %pad_maximum_fusion), channel_id=1, source_target_pairs={{0,1},{1,0},{2,3},{3,2},{4,5},{5,4},{6,7},{7,6},{8,9},{9,8},{10,11... | collective-permute-start | bytes 28311560 | tf_op jit(solution)/shard_map/ppermute | solution.py:72
  112.0 36.9 %collective-permute-start.6 = (bf16[3,128,2048]{2,1,0:T(8,128)(2,1)S(1)}, bf16[3,128,2048]{2,1,0:T(8,128)(2,1)S(1)}, u32[]{:S(2)}, u32[]{:S(2)}) collective-permute-start(bf16[3,128,2048]{2,1,0:T(8,128)(2,1)S(1)} %slice.443), channel_id=1, source_target_pairs={{0,2},{1,3},{2,0},{3,1},{4,6},{5,7},{6,4},{7,5},{8,10},{9,11},{10,... | collective-permute-start | bytes 4718600 | tf_op jit(solution)/shard_map/ppermute | solution.py:72
  115.1 36.6 %collective-permute-start.7 = (bf16[3,128,2048]{2,1,0:T(8,128)(2,1)S(1)}, bf16[3,128,2048]{2,1,0:T(8,128)(2,1)S(1)}, u32[]{:S(2)}, u32[]{:S(2)}) collective-permute-start(bf16[3,128,2048]{2,1,0:T(8,128)(2,1)S(1)} %slice.444), channel_id=1, source_target_pairs={{0,4},{1,5},{2,6},{3,7},{4,0},{5,1},{6,2},{7,3},{8,12},{9,13},{10,... | collective-permute-start | bytes 4718600 | tf_op jit(solution)/shard_map/ppermute | solution.py:72
  153.0 779.2 %all-reduce.9.cloned.1.call-start = ((), (), s32[]{:S(2)}) async-start(), calls=%async_computation.1 | async-start | bytes 8388608 | tf_op jit(solution)/shard_map/psum | solution.py:540
  215.3 26.7 %collective-permute-start.10 = (bf16[256,2048]{1,0:T(8,128)(2,1)}, bf16[256,2048]{1,0:T(8,128)(2,1)S(1)}, u32[]{:S(2)}, u32[]{:S(2)}) collective-permute-start(bf16[256,2048]{1,0:T(8,128)(2,1)} %get-tuple-element.153), channel_id=1, source_target_pairs={{0,4},{1,5},{2,6},{3,7},{4,0},{5,1},{6,2},{7,3},{8,12},{9,13},{10,... | collective-permute-start | bytes 3145736 | tf_op jit(solution)/shard_map/ppermute | solution.py:72
  216.4 26.3 %collective-permute-start.9 = (bf16[256,2048]{1,0:T(8,128)(2,1)}, bf16[256,2048]{1,0:T(8,128)(2,1)}, u32[]{:S(2)}, u32[]{:S(2)}) collective-permute-start(bf16[256,2048]{1,0:T(8,128)(2,1)} %get-tuple-element.153), channel_id=1, source_target_pairs={{0,2},{1,3},{2,0},{3,1},{4,6},{5,7},{6,4},{7,5},{8,10},{9,11},{10,... | collective-permute-start | bytes 3145736 | tf_op jit(solution)/shard_map/ppermute | solution.py:72
  221.3 33.0 %collective-permute-start.17 = (bf16[256,1024]{1,0:T(8,128)(2,1)S(1)}, bf16[256,1024]{1,0:T(8,128)(2,1)}, u32[]{:S(2)}, u32[]{:S(2)}) collective-permute-start(bf16[256,1024]{1,0:T(8,128)(2,1)S(1)} %get-tuple-element.208), channel_id=1, source_target_pairs={{0,6},{1,7},{2,4},{3,5},{4,2},{5,3},{6,0},{7,1},{8,14},{9,15},{10,... | collective-permute-start | bytes 1572872 | tf_op jit(solution)/shard_map/ppermute | solution.py:72
  222.9 42.4 %collective-permute-start.15 = (bf16[256,1024]{1,0:T(8,128)(2,1)}, bf16[256,1024]{1,0:T(8,128)(2,1)}, u32[]{:S(2)}, u32[]{:S(2)}) collective-permute-start(bf16[256,1024]{1,0:T(8,128)(2,1)} %get-tuple-element.210), channel_id=1, source_target_pairs={{0,2},{1,3},{2,0},{3,1},{4,6},{5,7},{6,4},{7,5},{8,10},{9,11},{10,... | collective-permute-start | bytes 1572872 | tf_op jit(solution)/shard_map/ppermute | solution.py:72
  224.3 43.0 %collective-permute-start.16 = (bf16[256,1024]{1,0:T(8,128)(2,1)}, bf16[256,1024]{1,0:T(8,128)(2,1)}, u32[]{:S(2)}, u32[]{:S(2)}) collective-permute-start(bf16[256,1024]{1,0:T(8,128)(2,1)} %get-tuple-element.209), channel_id=1, source_target_pairs={{0,4},{1,5},{2,6},{3,7},{4,0},{5,1},{6,2},{7,3},{8,12},{9,13},{10,... | collective-permute-start | bytes 1572872 | tf_op jit(solution)/shard_map/ppermute | solution.py:72
  241.9 31.2 %collective-permute-start.18 = (bf16[256,1024]{1,0:T(8,128)(2,1)}, bf16[256,1024]{1,0:T(8,128)(2,1)}, u32[]{:S(2)}, u32[]{:S(2)}) collective-permute-start(bf16[256,1024]{1,0:T(8,128)(2,1)} %get-tuple-element.207), channel_id=1, source_target_pairs={{0,1},{1,0},{2,3},{3,2},{4,5},{5,4},{6,7},{7,6},{8,9},{9,8},{10,11... | collective-permute-start | bytes 1572872 | tf_op jit(solution)/shard_map/ppermute | solution.py:72
  245.8 68.0 %collective-permute-start.13 = (bf16[768,2048]{1,0:T(8,128)(2,1)}, bf16[768,2048]{1,0:T(8,128)(2,1)}, u32[]{:S(2)}, u32[]{:S(2)}) collective-permute-start(bf16[768,2048]{1,0:T(8,128)(2,1)} %pad_maximum_fusion.2), channel_id=1, source_target_pairs={{0,1},{1,0},{2,3},{3,2},{4,5},{5,4},{6,7},{7,6},{8,9},{9,8},{10,11... | collective-permute-start | bytes 9437192 | tf_op jit(solution)/shard_map/ppermute | solution.py:72
  254.4 20.6 %collective-permute-start.19 = (bf16[256,1024]{1,0:T(8,128)(2,1)}, bf16[256,1024]{1,0:T(8,128)(2,1)}, u32[]{:S(2)}, u32[]{:S(2)}) collective-permute-start(bf16[256,1024]{1,0:T(8,128)(2,1)} %get-tuple-element.206), channel_id=1, source_target_pairs={{0,3},{1,2},{2,1},{3,0},{4,7},{5,6},{6,5},{7,4},{8,11},{9,10},{10,... | collective-permute-start | bytes 1572872 | tf_op jit(solution)/shard_map/ppermute | solution.py:72
  265.3 25.1 %collective-permute-start.20 = (bf16[256,1024]{1,0:T(8,128)(2,1)}, bf16[256,1024]{1,0:T(8,128)(2,1)S(1)}, u32[]{:S(2)}, u32[]{:S(2)}) collective-permute-start(bf16[256,1024]{1,0:T(8,128)(2,1)} %get-tuple-element.205), channel_id=1, source_target_pairs={{0,5},{1,4},{2,7},{3,6},{4,1},{5,0},{6,3},{7,2},{8,13},{9,12},{10,... | collective-permute-start | bytes 1572872 | tf_op jit(solution)/shard_map/ppermute | solution.py:72
  267.3 23.9 %collective-permute-start.21 = (bf16[256,1024]{1,0:T(8,128)(2,1)}, bf16[256,1024]{1,0:T(8,128)(2,1)S(1)}, u32[]{:S(2)}, u32[]{:S(2)}) collective-permute-start(bf16[256,1024]{1,0:T(8,128)(2,1)} %get-tuple-element.204), channel_id=1, source_target_pairs={{0,7},{1,6},{2,5},{3,4},{4,3},{5,2},{6,1},{7,0},{8,15},{9,14},{10,... | collective-permute-start | bytes 1572872 | tf_op jit(solution)/shard_map/ppermute | solution.py:72
  352.2 25.5 %collective-permute-start.23 = (bf16[256,2048]{1,0:T(8,128)(2,1)S(1)}, bf16[256,2048]{1,0:T(8,128)(2,1)S(1)}, u32[]{:S(2)}, u32[]{:S(2)}) collective-permute-start(bf16[256,2048]{1,0:T(8,128)(2,1)S(1)} %pad_maximum_fusion.13), channel_id=1, source_target_pairs={{0,2},{1,3},{2,0},{3,1},{4,6},{5,7},{6,4},{7,5},{8,10},{9,11},{10,... | collective-permute-start | bytes 3145736 | tf_op jit(solution)/shard_map/ppermute | solution.py:72
  352.8 25.7 %collective-permute-start.25 = (bf16[256,2048]{1,0:T(8,128)(2,1)S(1)}, bf16[256,2048]{1,0:T(8,128)(2,1)S(1)}, u32[]{:S(2)}, u32[]{:S(2)}) collective-permute-start(bf16[256,2048]{1,0:T(8,128)(2,1)S(1)} %pad_maximum_fusion.14), channel_id=1, source_target_pairs={{0,4},{1,5},{2,6},{3,7},{4,0},{5,1},{6,2},{7,3},{8,12},{9,13},{10,... | collective-permute-start | bytes 3145736 | tf_op jit(solution)/shard_map/ppermute | solution.py:72
  412.4 22.8 %collective-permute-start.28 = (bf16[256,2048]{1,0:T(8,128)(2,1)S(1)}, bf16[256,2048]{1,0:T(8,128)(2,1)S(1)}, u32[]{:S(2)}, u32[]{:S(2)}) collective-permute-start(bf16[256,2048]{1,0:T(8,128)(2,1)S(1)} %get-tuple-element.148), channel_id=1, source_target_pairs={{0,4},{1,5},{2,6},{3,7},{4,0},{5,1},{6,2},{7,3},{8,12},{9,13},{10,... | collective-permute-start | bytes 3145736 | tf_op jit(solution)/shard_map/ppermute | solution.py:72
  412.7 22.5 %collective-permute-start.27 = (bf16[256,2048]{1,0:T(8,128)(2,1)S(1)}, bf16[256,2048]{1,0:T(8,128)(2,1)S(1)}, u32[]{:S(2)}, u32[]{:S(2)}) collective-permute-start(bf16[256,2048]{1,0:T(8,128)(2,1)S(1)} %get-tuple-element.148), channel_id=1, source_target_pairs={{0,2},{1,3},{2,0},{3,1},{4,6},{5,7},{6,4},{7,5},{8,10},{9,11},{10,... | collective-permute-start | bytes 3145736 | tf_op jit(solution)/shard_map/ppermute | solution.py:72
  435.7 16.0 %collective-permute-start.31 = (bf16[768,2048]{1,0:T(8,128)(2,1)S(1)}, bf16[768,2048]{1,0:T(8,128)(2,1)S(1)}, u32[]{:S(2)}, u32[]{:S(2)}) collective-permute-start(bf16[768,2048]{1,0:T(8,128)(2,1)S(1)} %pad_maximum_fusion.3), channel_id=1, source_target_pairs={{0,1},{1,0},{2,3},{3,2},{4,5},{5,4},{6,7},{7,6},{8,9},{9,8},{10,11... | collective-permute-start | bytes 9437192 | tf_op jit(solution)/shard_map/ppermute | solution.py:72
  509.1 25.8 %collective-permute-start.34 = (bf16[256,2048]{1,0:T(8,128)(2,1)}, bf16[256,2048]{1,0:T(8,128)(2,1)}, u32[]{:S(2)}, u32[]{:S(2)}) collective-permute-start(bf16[256,2048]{1,0:T(8,128)(2,1)} %pad_maximum_fusion.16), channel_id=1, source_target_pairs={{0,2},{1,3},{2,0},{3,1},{4,6},{5,7},{6,4},{7,5},{8,10},{9,11},{10,... | collective-permute-start | bytes 3145736 | tf_op jit(solution)/shard_map/ppermute | solution.py:72
  513.7 569.7 %all-reduce.11.cloned.1.call-start = ((), (), s32[]{:S(2)}) async-start(), calls=%async_computation.2 | async-start | bytes 4194304 | tf_op jit(solution)/shard_map/psum | solution.py:545
  514.9 35.6 %collective-permute-start.36 = (bf16[256,2048]{1,0:T(8,128)(2,1)S(1)}, bf16[256,2048]{1,0:T(8,128)(2,1)S(1)}, u32[]{:S(2)}, u32[]{:S(2)}) collective-permute-start(bf16[256,2048]{1,0:T(8,128)(2,1)S(1)} %pad_maximum_fusion.17), channel_id=1, source_target_pairs={{0,4},{1,5},{2,6},{3,7},{4,0},{5,1},{6,2},{7,3},{8,12},{9,13},{10,... | collective-permute-start | bytes 3145736 | tf_op jit(solution)/shard_map/ppermute | solution.py:72
  536.4 19.3 %collective-permute-start.35 = (bf16[128,2048]{1,0:T(8,128)(2,1)S(1)}, bf16[128,2048]{1,0:T(8,128)(2,1)S(1)}, u32[]{:S(2)}, u32[]{:S(2)}) collective-permute-start(bf16[128,2048]{1,0:T(8,128)(2,1)S(1)} %fusion.92), channel_id=1, source_target_pairs={{0,4},{1,5},{2,6},{3,7},{4,0},{5,1},{6,2},{7,3},{8,12},{9,13},{10,... | collective-permute-start | bytes 1572872 | tf_op jit(solution)/shard_map/ppermute | solution.py:72
  553.4 25.7 %collective-permute-start.54 = (bf16[256,1024]{1,0:T(8,128)(2,1)S(1)}, bf16[256,1024]{1,0:T(8,128)(2,1)S(1)}, u32[]{:S(2)}, u32[]{:S(2)}) collective-permute-start(bf16[256,1024]{1,0:T(8,128)(2,1)S(1)} %get-tuple-element.172), channel_id=1, source_target_pairs={{0,4},{1,5},{2,6},{3,7},{4,0},{5,1},{6,2},{7,3},{8,12},{9,13},{10,... | collective-permute-start | bytes 1572872 | tf_op jit(solution)/shard_map/ppermute | solution.py:72
  555.2 23.9 %collective-permute-start.53 = (bf16[256,1024]{1,0:T(8,128)(2,1)S(1)}, bf16[256,1024]{1,0:T(8,128)(2,1)S(1)}, u32[]{:S(2)}, u32[]{:S(2)}) collective-permute-start(bf16[256,1024]{1,0:T(8,128)(2,1)S(1)} %get-tuple-element.173), channel_id=1, source_target_pairs={{0,2},{1,3},{2,0},{3,1},{4,6},{5,7},{6,4},{7,5},{8,10},{9,11},{10,... | collective-permute-start | bytes 1572872 | tf_op jit(solution)/shard_map/ppermute | solution.py:72
  555.5 154.8 %collective-permute-start.52 = (bf16[256,1024]{1,0:T(8,128)(2,1)}, bf16[256,1024]{1,0:T(8,128)(2,1)}, u32[]{:S(2)}, u32[]{:S(2)}) collective-permute-start(bf16[256,1024]{1,0:T(8,128)(2,1)} %get-tuple-element.174), channel_id=1, source_target_pairs={{0,7},{1,6},{2,5},{3,4},{4,3},{5,2},{6,1},{7,0},{8,15},{9,14},{10,... | collective-permute-start | bytes 1572872 | tf_op jit(solution)/shard_map/ppermute | solution.py:72
  555.8 34.5 %collective-permute-start.49 = (bf16[256,1024]{1,0:T(8,128)(2,1)S(1)}, bf16[256,1024]{1,0:T(8,128)(2,1)S(1)}, u32[]{:S(2)}, u32[]{:S(2)}) collective-permute-start(bf16[256,1024]{1,0:T(8,128)(2,1)S(1)} %get-tuple-element.177), channel_id=1, source_target_pairs={{0,1},{1,0},{2,3},{3,2},{4,5},{5,4},{6,7},{7,6},{8,9},{9,8},{10,11... | collective-permute-start | bytes 1572872 | tf_op jit(solution)/shard_map/ppermute | solution.py:72
  567.8 140.5 %collective-permute-start.51 = (bf16[256,1024]{1,0:T(8,128)(2,1)}, bf16[256,1024]{1,0:T(8,128)(2,1)}, u32[]{:S(2)}, u32[]{:S(2)}) collective-permute-start(bf16[256,1024]{1,0:T(8,128)(2,1)} %get-tuple-element.175), channel_id=1, source_target_pairs={{0,5},{1,4},{2,7},{3,6},{4,1},{5,0},{6,3},{7,2},{8,13},{9,12},{10,... | collective-permute-start | bytes 1572872 | tf_op jit(solution)/shard_map/ppermute | solution.py:72
  579.1 18.2 %collective-permute-start.50 = (bf16[256,1024]{1,0:T(8,128)(2,1)S(1)}, bf16[256,1024]{1,0:T(8,128)(2,1)S(1)}, u32[]{:S(2)}, u32[]{:S(2)}) collective-permute-start(bf16[256,1024]{1,0:T(8,128)(2,1)S(1)} %get-tuple-element.176), channel_id=1, source_target_pairs={{0,3},{1,2},{2,1},{3,0},{4,7},{5,6},{6,5},{7,4},{8,11},{9,10},{10,... | collective-permute-start | bytes 1572872 | tf_op jit(solution)/shard_map/ppermute | solution.py:72
  579.1 31.6 %collective-permute-start.37 = (bf16[128,2048]{1,0:T(8,128)(2,1)S(1)}, bf16[128,2048]{1,0:T(8,128)(2,1)S(1)}, u32[]{:S(2)}, u32[]{:S(2)}) collective-permute-start(bf16[128,2048]{1,0:T(8,128)(2,1)S(1)} %get-tuple-element.193), channel_id=1, source_target_pairs={{0,2},{1,3},{2,0},{3,1},{4,6},{5,7},{6,4},{7,5},{8,10},{9,11},{10,... | collective-permute-start | bytes 1572872 | tf_op jit(solution)/shard_map/ppermute | solution.py:72
  590.3 88.4 %collective-permute-start.56 = (bf16[256,4096]{1,0:T(8,128)(2,1)}, bf16[256,4096]{1,0:T(8,128)(2,1)}, u32[]{:S(2)}, u32[]{:S(2)}) collective-permute-start(bf16[256,4096]{1,0:T(8,128)(2,1)} %pad_maximum_fusion.8), channel_id=1, source_target_pairs={{0,8},{24,16},{1,9},{25,17},{2,10},{26,18},{3,11},{27,19},{4,12},{... | collective-permute-start | bytes 6291464 | tf_op jit(solution)/shard_map/ppermute | solution.py:177
  662.7 145.0 %collective-permute-start.40 = (bf16[1024,2048]{1,0:T(8,128)(2,1)}, bf16[1024,2048]{1,0:T(8,128)(2,1)}, u32[]{:S(2)}, u32[]{:S(2)}) collective-permute-start(bf16[1024,2048]{1,0:T(8,128)(2,1)} %convolution_convert_fusion.1), channel_id=1, source_target_pairs={{0,1},{1,0},{2,3},{3,2},{4,5},{5,4},{6,7},{7,6},{8,9},{9,8},{10,11... | collective-permute-start | bytes 12582920 | tf_op jit(solution)/shard_map/ppermute | solution.py:72
  675.3 39.0 %collective-permute-start.83 = (f32[35,2048]{1,0:T(8,128)S(1)}, f32[35,2048]{1,0:T(8,128)S(1)}, u32[]{:S(2)}, u32[]{:S(2)}) collective-permute-start(f32[35,2048]{1,0:T(8,128)S(1)} %fusion.171), channel_id=1, source_target_pairs={{0,2},{1,3},{2,0},{3,1},{4,6},{5,7},{6,4},{7,5},{8,10},{9,11},{10,... | collective-permute-start | bytes 860168 | tf_op jit(solution)/shard_map/ppermute | solution.py:72
  682.4 117.1 %collective-permute-start.59 = (bf16[256,4096]{1,0:T(8,128)(2,1)}, bf16[256,4096]{1,0:T(8,128)(2,1)}, u32[]{:S(2)}, u32[]{:S(2)}) collective-permute-start(bf16[256,4096]{1,0:T(8,128)(2,1)} %fusion.8), channel_id=1, source_target_pairs={{8,16},{16,8},{9,17},{17,9},{10,18},{18,10},{11,19},{19,11},{12,20... | collective-permute-start | bytes 6291464 | tf_op jit(solution)/shard_map/ppermute | solution.py:177
  727.1 76.2 %collective-permute-start.57 = (bf16[256,4096]{1,0:T(8,128)(2,1)}, bf16[256,4096]{1,0:T(8,128)(2,1)}, u32[]{:S(2)}, u32[]{:S(2)}) collective-permute-start(bf16[256,4096]{1,0:T(8,128)(2,1)} %constant_dynamic-update-slice_fusion.31), channel_id=1, source_target_pairs={{0,8},{24,16},{1,9},{25,17},{2,10},{26,18},{3,11},{27,19},{4,12},{... | collective-permute-start | bytes 6291464 | tf_op jit(solution)/shard_map/ppermute | solution.py:177
  733.8 80.9 %collective-permute-start.39 = (bf16[1024,2048]{1,0:T(8,128)(2,1)}, bf16[1024,2048]{1,0:T(8,128)(2,1)}, u32[]{:S(2)}, u32[]{:S(2)}) collective-permute-start(bf16[1024,2048]{1,0:T(8,128)(2,1)} %convolution_convert_fusion.2), channel_id=1, source_target_pairs={{0,1},{1,0},{2,3},{3,2},{4,5},{5,4},{6,7},{7,6},{8,9},{9,8},{10,11... | collective-permute-start | bytes 12582920 | tf_op jit(solution)/shard_map/ppermute | solution.py:72
  735.3 43.5 %collective-permute-start.81 = (f32[3,2048]{1,0:T(4,128)S(1)}, f32[3,2048]{1,0:T(4,128)S(1)}, u32[]{:S(2)}, u32[]{:S(2)}) collective-permute-start(f32[3,2048]{1,0:T(4,128)S(1)} %add.538), channel_id=1, source_target_pairs={{0,16},{8,24},{16,0},{24,8},{1,17},{9,25},{17,1},{25,9},{2,18},{10... | collective-permute-start | bytes 73736 | tf_op jit(solution)/shard_map/ppermute | solution.py:150
  778.8 16.3 %collective-permute-start.86 = (f32[35,2048]{1,0:T(8,128)S(1)}, f32[35,2048]{1,0:T(8,128)S(1)}, u32[]{:S(2)}, u32[]{:S(2)}) collective-permute-start(f32[35,2048]{1,0:T(8,128)S(1)} %add.551), channel_id=1, source_target_pairs={{0,16},{8,24},{16,0},{24,8},{1,17},{9,25},{17,1},{25,9},{2,18},{10... | collective-permute-start | bytes 860168 | tf_op jit(solution)/shard_map/ppermute | solution.py:150
  795.1 24.5 %collective-permute-start.65 = (bf16[1024,2048]{1,0:T(8,128)(2,1)}, bf16[1024,2048]{1,0:T(8,128)(2,1)}, u32[]{:S(2)}, u32[]{:S(2)}) collective-permute-start(bf16[1024,2048]{1,0:T(8,128)(2,1)} %convolution_convert_fusion), channel_id=1, source_target_pairs={{0,1},{1,0},{2,3},{3,2},{4,5},{5,4},{6,7},{7,6},{8,9},{9,8},{10,11... | collective-permute-start | bytes 12582920 | tf_op jit(solution)/shard_map/ppermute | solution.py:72
  799.5 26.2 %collective-permute-start.38 = (bf16[1024,2048]{1,0:T(8,128)(2,1)}, bf16[1024,2048]{1,0:T(8,128)(2,1)S(1)}, u32[]{:S(2)}, u32[]{:S(2)}) collective-permute-start(bf16[1024,2048]{1,0:T(8,128)(2,1)} %convolution_convert_fusion.3), channel_id=1, source_target_pairs={{0,1},{1,0},{2,3},{3,2},{4,5},{5,4},{6,7},{7,6},{8,9},{9,8},{10,11... | collective-permute-start | bytes 12582920 | tf_op jit(solution)/shard_map/ppermute | solution.py:72
  803.3 60.5 %collective-permute-start.62 = (bf16[256,4096]{1,0:T(8,128)(2,1)S(1)}, bf16[256,4096]{1,0:T(8,128)(2,1)S(1)}, u32[]{:S(2)}, u32[]{:S(2)}) collective-permute-start(bf16[256,4096]{1,0:T(8,128)(2,1)S(1)} %fusion.30), channel_id=1, source_target_pairs={{8,0},{16,24},{9,1},{17,25},{10,2},{18,26},{11,3},{19,27},{12,4},{... | collective-permute-start | bytes 6291464 | tf_op jit(solution)/shard_map/ppermute | solution.py:177
  807.8 50.6 %collective-permute-start.60 = (bf16[256,4096]{1,0:T(8,128)(2,1)S(1)}, bf16[256,4096]{1,0:T(8,128)(2,1)S(1)}, u32[]{:S(2)}, u32[]{:S(2)}) collective-permute-start(bf16[256,4096]{1,0:T(8,128)(2,1)S(1)} %fusion.7), channel_id=1, source_target_pairs={{8,16},{16,8},{9,17},{17,9},{10,18},{18,10},{11,19},{19,11},{12,20... | collective-permute-start | bytes 6291464 | tf_op jit(solution)/shard_map/ppermute | solution.py:177
  814.7 25.4 %collective-permute-start.41 = (bf16[256,2048]{1,0:T(8,128)(2,1)}, bf16[256,2048]{1,0:T(8,128)(2,1)}, u32[]{:S(2)}, u32[]{:S(2)}) collective-permute-start(bf16[256,2048]{1,0:T(8,128)(2,1)} %pad_maximum_fusion.20), channel_id=1, source_target_pairs={{0,2},{1,3},{2,0},{3,1},{4,6},{5,7},{6,4},{7,5},{8,10},{9,11},{10,... | collective-permute-start | bytes 3145736 | tf_op jit(solution)/shard_map/ppermute | solution.py:72
  819.5 26.1 %collective-permute-start.42 = (bf16[256,2048]{1,0:T(8,128)(2,1)}, bf16[256,2048]{1,0:T(8,128)(2,1)S(1)}, u32[]{:S(2)}, u32[]{:S(2)}) collective-permute-start(bf16[256,2048]{1,0:T(8,128)(2,1)} %pad_maximum_fusion.21), channel_id=1, source_target_pairs={{0,4},{1,5},{2,6},{3,7},{4,0},{5,1},{6,2},{7,3},{8,12},{9,13},{10,... | collective-permute-start | bytes 3145736 | tf_op jit(solution)/shard_map/ppermute | solution.py:72
  845.7 26.1 %collective-permute-start.43 = (bf16[256,2048]{1,0:T(8,128)(2,1)S(1)}, bf16[256,2048]{1,0:T(8,128)(2,1)S(1)}, u32[]{:S(2)}, u32[]{:S(2)}) collective-permute-start(bf16[256,2048]{1,0:T(8,128)(2,1)S(1)} %pad_maximum_fusion.19), channel_id=1, source_target_pairs={{0,2},{1,3},{2,0},{3,1},{4,6},{5,7},{6,4},{7,5},{8,10},{9,11},{10,... | collective-permute-start | bytes 3145736 | tf_op jit(solution)/shard_map/ppermute | solution.py:72
  846.1 32.2 %collective-permute-start.44 = (bf16[256,2048]{1,0:T(8,128)(2,1)S(1)}, bf16[256,2048]{1,0:T(8,128)(2,1)S(1)}, u32[]{:S(2)}, u32[]{:S(2)}) collective-permute-start(bf16[256,2048]{1,0:T(8,128)(2,1)S(1)} %pad_maximum_fusion.22), channel_id=1, source_target_pairs={{0,4},{1,5},{2,6},{3,7},{4,0},{5,1},{6,2},{7,3},{8,12},{9,13},{10,... | collective-permute-start | bytes 3145736 | tf_op jit(solution)/shard_map/ppermute | solution.py:72
  857.3 48.1 %collective-permute-start.74 = (bf16[128,2048]{1,0:T(8,128)(2,1)S(1)}, bf16[128,2048]{1,0:T(8,128)(2,1)S(1)}, u32[]{:S(2)}, u32[]{:S(2)}) collective-permute-start(bf16[128,2048]{1,0:T(8,128)(2,1)S(1)} %get-tuple-element.161), channel_id=1, source_target_pairs={{0,2},{1,3},{2,0},{3,1},{4,6},{5,7},{6,4},{7,5},{8,10},{9,11},{10,... | collective-permute-start | bytes 1572872 | tf_op jit(solution)/shard_map/ppermute | solution.py:72
  863.8 98.8 %collective-permute-start.63 = (bf16[256,4096]{1,0:T(8,128)(2,1)}, bf16[256,4096]{1,0:T(8,128)(2,1)}, u32[]{:S(2)}, u32[]{:S(2)}) collective-permute-start(bf16[256,4096]{1,0:T(8,128)(2,1)} %fusion.29), channel_id=1, source_target_pairs={{8,0},{16,24},{9,1},{17,25},{10,2},{18,26},{11,3},{19,27},{12,4},{... | collective-permute-start | bytes 6291464 | tf_op jit(solution)/shard_map/ppermute | solution.py:177
  878.3 26.1 %collective-permute-start.45 = (bf16[256,2048]{1,0:T(8,128)(2,1)S(1)}, bf16[256,2048]{1,0:T(8,128)(2,1)S(1)}, u32[]{:S(2)}, u32[]{:S(2)}) collective-permute-start(bf16[256,2048]{1,0:T(8,128)(2,1)S(1)} %pad_maximum_fusion.18), channel_id=1, source_target_pairs={{0,2},{1,3},{2,0},{3,1},{4,6},{5,7},{6,4},{7,5},{8,10},{9,11},{10,... | collective-permute-start | bytes 3145736 | tf_op jit(solution)/shard_map/ppermute | solution.py:72
  884.5 32.5 %collective-permute-start.47 = (bf16[256,2048]{1,0:T(8,128)(2,1)S(1)}, bf16[256,2048]{1,0:T(8,128)(2,1)S(1)}, u32[]{:S(2)}, u32[]{:S(2)}) collective-permute-start(bf16[256,2048]{1,0:T(8,128)(2,1)S(1)} %pad_maximum_fusion.23), channel_id=1, source_target_pairs={{0,4},{1,5},{2,6},{3,7},{4,0},{5,1},{6,2},{7,3},{8,12},{9,13},{10,... | collective-permute-start | bytes 3145736 | tf_op jit(solution)/shard_map/ppermute | solution.py:72
  894.9 23.7 %collective-permute-start.76 = (bf16[128,2048]{1,0:T(8,128)(2,1)S(1)}, bf16[128,2048]{1,0:T(8,128)(2,1)S(1)}, u32[]{:S(2)}, u32[]{:S(2)}) collective-permute-start(bf16[128,2048]{1,0:T(8,128)(2,1)S(1)} %get-tuple-element.163), channel_id=1, source_target_pairs={{0,2},{1,3},{2,0},{3,1},{4,6},{5,7},{6,4},{7,5},{8,10},{9,11},{10,... | collective-permute-start | bytes 1572872 | tf_op jit(solution)/shard_map/ppermute | solution.py:72
  904.8 23.4 %collective-permute-start.46 = (bf16[128,2048]{1,0:T(8,128)(2,1)S(1)}, bf16[128,2048]{1,0:T(8,128)(2,1)S(1)}, u32[]{:S(2)}, u32[]{:S(2)}) collective-permute-start(bf16[128,2048]{1,0:T(8,128)(2,1)S(1)} %fusion.87), channel_id=1, source_target_pairs={{0,4},{1,5},{2,6},{3,7},{4,0},{5,1},{6,2},{7,3},{8,12},{9,13},{10,... | collective-permute-start | bytes 1572872 | tf_op jit(solution)/shard_map/ppermute | solution.py:72
  917.0 26.4 %collective-permute-start.66 = (bf16[256,2048]{1,0:T(8,128)(2,1)}, bf16[256,2048]{1,0:T(8,128)(2,1)}, u32[]{:S(2)}, u32[]{:S(2)}) collective-permute-start(bf16[256,2048]{1,0:T(8,128)(2,1)} %pad_maximum_fusion.25), channel_id=1, source_target_pairs={{0,2},{1,3},{2,0},{3,1},{4,6},{5,7},{6,4},{7,5},{8,10},{9,11},{10,... | collective-permute-start | bytes 3145736 | tf_op jit(solution)/shard_map/ppermute | solution.py:72
  918.1 38.8 %collective-permute-start.68 = (bf16[256,2048]{1,0:T(8,128)(2,1)}, bf16[256,2048]{1,0:T(8,128)(2,1)}, u32[]{:S(2)}, u32[]{:S(2)}) collective-permute-start(bf16[256,2048]{1,0:T(8,128)(2,1)} %pad_maximum_fusion.26), channel_id=1, source_target_pairs={{0,4},{1,5},{2,6},{3,7},{4,0},{5,1},{6,2},{7,3},{8,12},{9,13},{10,... | collective-permute-start | bytes 3145736 | tf_op jit(solution)/shard_map/ppermute | solution.py:72
  929.5 19.8 %collective-permute-start.48 = (bf16[128,2048]{1,0:T(8,128)(2,1)}, bf16[128,2048]{1,0:T(8,128)(2,1)}, u32[]{:S(2)}, u32[]{:S(2)}) collective-permute-start(bf16[128,2048]{1,0:T(8,128)(2,1)} %get-tuple-element.179), channel_id=1, source_target_pairs={{0,2},{1,3},{2,0},{3,1},{4,6},{5,7},{6,4},{7,5},{8,10},{9,11},{10,... | collective-permute-start | bytes 1572872 | tf_op jit(solution)/shard_map/ppermute | solution.py:72
  950.7 44.0 %collective-permute-start.58 = (bf16[256,2048]{1,0:T(8,128)(2,1)S(1)}, bf16[256,2048]{1,0:T(8,128)(2,1)S(1)}, u32[]{:S(2)}, u32[]{:S(2)}) collective-permute-start(bf16[256,2048]{1,0:T(8,128)(2,1)S(1)} %pad_maximum_fusion.24), channel_id=1, source_target_pairs={{0,8},{24,16},{1,9},{25,17},{2,10},{26,18},{3,11},{27,19},{4,12},{... | collective-permute-start | bytes 3145736 | tf_op jit(solution)/shard_map/ppermute | solution.py:177
  994.8 43.6 %collective-permute-start.70 = (bf16[256,2048]{1,0:T(8,128)(2,1)S(1)}, bf16[256,2048]{1,0:T(8,128)(2,1)S(1)}, u32[]{:S(2)}, u32[]{:S(2)}) collective-permute-start(bf16[256,2048]{1,0:T(8,128)(2,1)S(1)} %pad_maximum_fusion.27), channel_id=1, source_target_pairs={{0,8},{24,16},{1,9},{25,17},{2,10},{26,18},{3,11},{27,19},{4,12},{... | collective-permute-start | bytes 3145736 | tf_op jit(solution)/shard_map/ppermute | solution.py:177
  999.6 39.1 %collective-permute-start.61 = (bf16[256,2048]{1,0:T(8,128)(2,1)S(1)}, bf16[256,2048]{1,0:T(8,128)(2,1)S(1)}, u32[]{:S(2)}, u32[]{:S(2)}) collective-permute-start(bf16[256,2048]{1,0:T(8,128)(2,1)S(1)} %fusion.40), channel_id=1, source_target_pairs={{8,16},{16,8},{9,17},{17,9},{10,18},{18,10},{11,19},{19,11},{12,20... | collective-permute-start | bytes 3145736 | tf_op jit(solution)/shard_map/ppermute | solution.py:177
  1040.0 41.0 %collective-permute-start.64 = (bf16[256,2048]{1,0:T(8,128)(2,1)S(1)}, bf16[256,2048]{1,0:T(8,128)(2,1)S(1)}, u32[]{:S(2)}, u32[]{:S(2)}) collective-permute-start(bf16[256,2048]{1,0:T(8,128)(2,1)S(1)} %fusion.45), channel_id=1, source_target_pairs={{8,0},{16,24},{9,1},{17,25},{10,2},{18,26},{11,3},{19,27},{12,4},{... | collective-permute-start | bytes 3145736 | tf_op jit(solution)/shard_map/ppermute | solution.py:177
  1082.0 19.6 %collective-permute-start.72 = (bf16[256,2048]{1,0:T(8,128)(2,1)}, bf16[256,2048]{1,0:T(8,128)(2,1)}, u32[]{:S(2)}, u32[]{:S(2)}) collective-permute-start(bf16[256,2048]{1,0:T(8,128)(2,1)} %fusion.46), channel_id=1, source_target_pairs={{8,0},{16,24},{9,1},{17,25},{10,2},{18,26},{11,3},{19,27},{12,4},{... | collective-permute-start | bytes 3145736 | tf_op jit(solution)/shard_map/ppermute | solution.py:177
  (153 other events, 2296.9 us)
Sparse Core Ops, SparseCore 0:
  153.1 53.7 all-gather.1
  513.8 193.0 all-reduce.8
  932.3 124.5 all-reduce.10
